TPU v7x, 128 devices: a whole 4x4x4 slice. The times are simulated.
128 devices in a mesh: blk: 32 (over x, y, core), head: 4 (over z).
Axes of the slice: x: 4, y: 4, z: 4, core: 2. Of those that a mesh axis runs over, the one named last changes fastest.
Arguments:
- queries: bfloat16 [8192, 512], P(('blk', 'head')), may hold values from -6 to 6
- keys: bfloat16 [8192, 512], P(('blk', 'head')), may hold values from -6 to 6
- values: bfloat16 [8192, 512], P(('blk', 'head')), may hold values from -6 to 6
- out_grad: bfloat16 [8192, 512], P(('blk', 'head')), may hold values from -6 to 6
- tile_mask: int32 [64, 64], replicated, may hold values from 0 to 1, as said below
- frame_order: int32 [32], replicated, may hold values from 0 to 31, each once
Outputs:
- query_grad: bfloat16 [8192, 512], P(('blk', 'head'))
- key_grad: bfloat16 [8192, 512], P(('blk', 'head'))
- value_grad: bfloat16 [8192, 512], P(('blk', 'head'))
Inputs may be any that keep to these rules, and one draw needn't show every extreme that they name: `tile_mask`: 1 where a query tile may attend a key tile, else 0; every tile may attend all tiles of its own frame. Shard b of blk holds frame frame_order[b]; each frame once.
All inputs are finite; a program needn't handle non-finite values.
Results may differ from a plain program's by a relative error of at most 0.0024.
The roundings to bfloat16 on the way count: a program that leaves them out, or rounds other values in their place, can miss the bound.
Values may be sent and summed in bfloat16 or wider, within the bound.
A program may use at most 64 MiB of HBM per device.

v0:
```python
import jax
import jax.numpy as jnp
from jax import lax
from jax.sharding import PartitionSpec as P

HDIM = 64
TILE = 128


NEGATIVE = -1e30


def token_tiles(frame_order, row_count):
    token_total = frame_order.shape[0] * row_count
    places = jnp.arange(token_total, dtype=jnp.int32)
    frames = jnp.take(frame_order, places // row_count)
    return frames * (row_count // TILE) + places % row_count // TILE


def split_heads(matrix, local_heads):
    return matrix.reshape(matrix.shape[0], local_heads, HDIM)


def raw_scores(query_part, key_part, local_heads):
    return jnp.einsum(
        "qhd,khd->hqk",
        split_heads(query_part, local_heads),
        split_heads(key_part, local_heads),
        preferred_element_type=jnp.float32,
    ) * HDIM ** (-0.5)


def key_terms(
    query_part, grad_part, log_mass, row_delta, key_part, value_part, allowed, local_heads
):
    scores = raw_scores(query_part, key_part, local_heads)
    probs_full = jnp.where(allowed[None], jnp.exp(scores - log_mass[:, :, None]), 0.0)
    prob_grad = jnp.einsum(
        "qhd,khd->hqk",
        split_heads(grad_part, local_heads),
        split_heads(value_part, local_heads),
        preferred_element_type=jnp.float32,
    )
    score_grad = (probs_full * (prob_grad - row_delta[:, :, None])).astype(jnp.bfloat16)
    probs_half = probs_full.astype(jnp.bfloat16)
    key_grad = jnp.einsum(
        "hqk,qhd->khd",
        score_grad,
        split_heads(query_part, local_heads),
        preferred_element_type=jnp.float32,
    )
    value_grad = jnp.einsum(
        "hqk,qhd->khd",
        probs_half,
        split_heads(grad_part, local_heads),
        preferred_element_type=jnp.float32,
    )
    return (key_grad, value_grad)


def body(queries, keys, values, out_grad, tile_mask, frame_order):
    query_local, key_local, value_local, grad_local = (
        lax.all_to_all(queries, "head", split_axis=1, concat_axis=0, tiled=True),
        lax.all_to_all(keys, "head", split_axis=1, concat_axis=0, tiled=True),
        lax.all_to_all(values, "head", split_axis=1, concat_axis=0, tiled=True),
        lax.all_to_all(out_grad, "head", split_axis=1, concat_axis=0, tiled=True),
    )
    row_count, feature_width = query_local.shape
    local_heads = feature_width // HDIM
    shard_count = lax.axis_size("blk")
    shard_index = lax.axis_index("blk")
    tiles = token_tiles(frame_order, row_count)
    my_tiles = lax.dynamic_slice_in_dim(tiles, shard_index * row_count, row_count, 0)
    my_mask = jnp.take(tile_mask, my_tiles, axis=0)
    group_size = 4
    block_rows = row_count * group_size
    turn_count = shard_count // group_size
    key_all, value_all = (
        lax.all_gather(key_local, "blk", axis=0, tiled=True),
        lax.all_gather(value_local, "blk", axis=0, tiled=True),
    )

    def sweep_keys(update, initial):

        def turn(turn_index, running):
            offset = turn_index * block_rows
            key_tiles = lax.dynamic_slice_in_dim(tiles, offset, block_rows, 0)
            allowed = jnp.take(my_mask, key_tiles, axis=1) == 1
            key_part = lax.dynamic_slice_in_dim(key_all, offset, block_rows, 0)
            value_part = lax.dynamic_slice_in_dim(value_all, offset, block_rows, 0)
            return update(running, key_part, value_part, allowed)

        return lax.fori_loop(0, turn_count, turn, initial)

    def add_mass(running, key_part, value_part, allowed):
        running_peak, running_mass = running
        scores = jnp.where(allowed[None], raw_scores(query_local, key_part, local_heads), NEGATIVE)
        new_peak = jnp.maximum(running_peak, jnp.max(scores, axis=2))
        exponent = jnp.where(allowed[None], jnp.exp(scores - new_peak[:, :, None]), 0.0)
        return (
            new_peak,
            running_mass * jnp.exp(running_peak - new_peak) + jnp.sum(exponent, axis=2),
        )

    stat_shape = (local_heads, row_count)
    running_peak, running_mass = sweep_keys(
        add_mass, (jnp.full(stat_shape, NEGATIVE, jnp.float32), jnp.zeros(stat_shape, jnp.float32))
    )
    log_mass = running_peak + jnp.log(running_mass)

    def add_output(running, key_part, value_part, allowed):
        scores = raw_scores(query_local, key_part, local_heads)
        probs_half = jnp.where(allowed[None], jnp.exp(scores - log_mass[:, :, None]), 0.0).astype(
            jnp.bfloat16
        )
        return running + jnp.einsum(
            "hqk,khd->qhd",
            probs_half,
            split_heads(value_part, local_heads),
            preferred_element_type=jnp.float32,
        )

    head_zeros = jnp.zeros((row_count, local_heads, HDIM), jnp.float32)
    attention_out = sweep_keys(add_output, head_zeros).astype(jnp.bfloat16)
    row_delta = jnp.sum(
        split_heads(grad_local, local_heads).astype(jnp.float32)
        * attention_out.astype(jnp.float32),
        axis=2,
    ).T

    def add_query_grad(running, key_part, value_part, allowed):
        scores = raw_scores(query_local, key_part, local_heads)
        probs_full = jnp.where(allowed[None], jnp.exp(scores - log_mass[:, :, None]), 0.0)
        prob_grad = jnp.einsum(
            "qhd,khd->hqk",
            split_heads(grad_local, local_heads),
            split_heads(value_part, local_heads),
            preferred_element_type=jnp.float32,
        )
        score_grad = (probs_full * (prob_grad - row_delta[:, :, None])).astype(jnp.bfloat16)
        return running + jnp.einsum(
            "hqk,khd->qhd",
            score_grad,
            split_heads(key_part, local_heads),
            preferred_element_type=jnp.float32,
        )

    query_grad = sweep_keys(add_query_grad, head_zeros)
    amount = row_count * lax.axis_size("blk")

    def one_part(turn_index):
        first_row = turn_index * block_rows
        key_part = lax.dynamic_slice_in_dim(key_all, first_row, block_rows, 0)
        value_part = lax.dynamic_slice_in_dim(value_all, first_row, block_rows, 0)
        key_tiles = lax.dynamic_slice_in_dim(tiles, first_row, block_rows, 0)
        allowed = jnp.take(my_mask, key_tiles, axis=1) == 1
        key_part_grad, value_part_grad = key_terms(
            query_local, grad_local, log_mass, row_delta, key_part, value_part, allowed, local_heads
        )
        return jnp.concatenate(
            [
                key_part_grad.reshape(block_rows, feature_width),
                value_part_grad.reshape(block_rows, feature_width),
            ],
            axis=1,
        )

    summed = lax.psum_scatter(
        lax.map(one_part, jnp.arange(amount // block_rows, dtype=jnp.int32)).reshape(
            amount, 2 * feature_width
        ),
        "blk",
        scatter_dimension=0,
        tiled=True,
    )
    key_sum = summed[:, :feature_width]
    value_sum = summed[:, feature_width:]
    score_scale = HDIM ** (-0.5)
    query_out = (query_grad * score_scale).reshape(row_count, feature_width).astype(jnp.bfloat16)
    key_out = (key_sum * score_scale).astype(jnp.bfloat16)
    value_out = value_sum.astype(jnp.bfloat16)
    return (
        lax.all_to_all(query_out, "head", split_axis=0, concat_axis=1, tiled=True),
        lax.all_to_all(key_out, "head", split_axis=0, concat_axis=1, tiled=True),
        lax.all_to_all(value_out, "head", split_axis=0, concat_axis=1, tiled=True),
    )


def solution(mesh):
    in_specs = (
        P(("blk", "head"), None),
        P(("blk", "head"), None),
        P(("blk", "head"), None),
        P(("blk", "head"), None),
        P(),
        P(),
    )
    out_specs = (P(("blk", "head"), None), P(("blk", "head"), None), P(("blk", "head"), None))
    return jax.shard_map(body, mesh=mesh, in_specs=in_specs, out_specs=out_specs, check_vma=False)
```

profile of v0, /device:TPU:0, one launch (start us, length us, event | category | flops | bytes accessed | tf_op | source)
XLA Modules:
  0.0 369.3 jit_solution(6514238794050728768)
XLA Ops:
  8.0 10.9 %all_to_all.130 = bf16[64,4,128]{2,0,1:T(8,128)(2,1)} all-to-all(bf16[64,4,128]{2,0,1:T(8,128)(2,1)S(1)} %copy_bitcast_fusion.6), channel_id=1, replica_groups=mesh['blk'=32,'head'=4] {'head'}, dimensions={1} | all-to-all | bytes 131072 | tf_op jit(solution)/shard_map/all_to_all | solution.py:64
  29.1 4.3 %compare_select_fusion.5 = s32[8192,1]{0,1:T(1,128)S(1)} fusion(s32[]{:T(128)} %bitcast.40, s32[]{:T(128)} %bitcast.41, s32[]{:T(128)} %bitcast.42, s32[]{:T(128)} %bitcast.43, s32[]{:T(128)} %bitcast.44, s32[]{:T(128)} %bitcast.46, s32[]{:T(128)} %bitcast.45), kind=kLoop, calls=%fused_computation.99 | loop fusion | flops 188416 | bytes 32796 | tf_op jit(solution)/shard_map/jit(_take)/gather | solution.py:16
  33.4 15.9 %fusion.41 = s32[8192]{0:T(1024)S(1)} fusion(pred[8192]{0:T(1024)(128)(4,1)S(1)} %compare_reduce_fusion, pred[8192]{0:T(1024)(128)(4,1)S(1)} %compare_reduce_fusion.1, pred[8192]{0:T(1024)(128)(4,1)S(1)} %compare_reduce_fusion.2, pred[8192]{0:T(1024)(128)(4,1)S(1)} %compare_reduce_fusion.3, pred[8192]{0:T(1024)(128)(4,1)S(1)} %compare_reduce_fusion.4, ...), kind=kLoop, calls=%fused_computation.134 | loop fusion | flops 499712 | bytes 270436 | tf_op jit(solution)/shard_map/add | solution.py:17
  51.7 4.7 %all-to-all-start.3 = ((bf16[64,4,128]{2,0,1:T(8,128)(2,1)}), bf16[64,4,128]{2,0,1:T(8,128)(2,1)S(1)}, u32[]{:S(2)}, u32[]{:S(2)}) async-start(bf16[64,4,128]{2,0,1:T(8,128)(2,1)} %copy_bitcast_fusion.3), calls=%async_computation.3 | async-start | bytes 131072 | tf_op jit(solution)/shard_map/all_to_all | solution.py:66
  57.1 4.9 %all-to-all-done.3 = bf16[64,4,128]{2,0,1:T(8,128)(2,1)S(1)} async-done(((bf16[64,4,128]{2,0,1:T(8,128)(2,1)}), bf16[64,4,128]{2,0,1:T(8,128)(2,1)S(1)}, u32[]{:S(2)}, u32[]{:S(2)}) %all-to-all-start.3) | async-done | bytes 65568 | tf_op jit(solution)/shard_map/all_to_all | solution.py:66
  65.8 5.1 %all-to-all-done.2 = bf16[64,4,128]{2,0,1:T(8,128)(2,1)S(1)} async-done(((bf16[64,4,128]{2,0,1:T(8,128)(2,1)}), bf16[64,4,128]{2,0,1:T(8,128)(2,1)S(1)}, u32[]{:S(2)}, u32[]{:S(2)}) %all-to-all-start.2) | async-done | bytes 65568 | tf_op jit(solution)/shard_map/all_to_all | solution.py:65
  71.6 4.1 %copy.123 = bf16[8192,128]{0,1:T(8,128)(2,1)} copy(bf16[8192,128]{1,0:T(8,128)(2,1)} %all-gather.3.cloned.1.call-done) | data formatting | bytes 4194304
  75.7 47.5 %while.55 = (s32[]{:T(128)}, f32[2,256]{1,0:T(2,128)S(1)}, f32[2,256]{1,0:T(2,128)S(1)}, s32[8192]{0:T(1024)S(1)}, s32[256,64]{0,1:T(8,128)S(1)}, /*index=5*/bf1...) while((s32[]{:T(128)}, f32[2,256]{1,0:T(2,128)S(1)}, ...), condition=%wide.region_3.5_spmd.clone, body=%wide.region_0.4_spmd.clone.sunk | while | flops 71840264 | bytes 9023666 | solution.py:93
  81.7 3.5 gather_fusion.1
  87.6 3.5 gather_fusion.1
  93.6 3.5 gather_fusion.1
  99.5 3.5 gather_fusion.1
  105.4 3.5 gather_fusion.1
  111.4 3.5 gather_fusion.1
  117.3 3.5 gather_fusion.1
  123.3 4.1 %copy.126 = bf16[8192,128]{0,1:T(8,128)(2,1)} copy(bf16[8192,128]{1,0:T(8,128)(2,1)} %all-gather.5.cloned.1.call-done) | data formatting | bytes 4194304
  127.4 45.7 %while.56 = (s32[]{:T(128)}, f32[256,2,64]{0,2,1:T(8,128)S(1)}, bf16[8192,128]{0,1:T(8,128)(2,1)}, s32[8192]{0:T(1024)S(1)}, s32[256,64]{0,1:T(8,128)S(1)}, /*in...) while((s32[]{:T(128)}, f32[256,2,64]{0,2,1:T(8,128)S(1)}, ...), condition=%wide.region_5.7_spmd.clone, body=%wide.region_4.6_spmd.clone.sunk | while | flops 136914944 | bytes 5591225 | solution.py:93
  133.1 3.5 gather_fusion.2
  138.8 3.5 gather_fusion.2
  144.5 3.5 gather_fusion.2
  150.3 3.5 gather_fusion.2
  156.0 3.5 gather_fusion.2
  161.7 3.5 gather_fusion.2
  173.7 75.7 %while.54 = (s32[]{:T(128)}, f32[8,1024,256]{2,1,0:T(8,128)}, s32[8]{0:T(128)S(1)}, s32[8192]{0:T(1024)S(1)}, s32[256,64]{0,1:T(8,128)S(1)}, /*index=5*/bf16[819...) while((s32[]{:T(128)}, f32[8,1024,256]{2,1,0:T(8,128)}, ...), condition=%wide.region_10.12_spmd, body=%wide.region_9.11_spmd.sunk | while | flops 272902144 | bytes 19159764 | solution.py:169
  212.8 3.5 gather_fusion
  249.4 51.0 %while.57 = (s32[]{:T(128)}, f32[256,2,64]{0,2,1:T(8,128)S(1)}, bf16[8192,128]{0,1:T(8,128)(2,1)}, s32[8192]{0:T(1024)S(1)}, s32[256,64]{0,1:T(8,128)S(1)}, /*in...) while((s32[]{:T(128)}, f32[256,2,64]{0,2,1:T(8,128)S(1)}, ...), condition=%wide.region_8.10_spmd.clone, body=%wide.region_7.9_spmd.clone.sunk | while | flops 205072384 | bytes 10115273 | solution.py:93
  262.2 3.5 gather_fusion.3
  300.6 8.0 %all_to_all.131 = bf16[4,64,128]{2,1,0:T(8,128)(2,1)S(1)} all-to-all(bf16[4,64,128]{2,1,0:T(8,128)(2,1)S(1)} %copy.144), channel_id=1, replica_groups=mesh['blk'=32,'head'=4] {'head'}, dimensions={0} | all-to-all | bytes 131072 | tf_op jit(solution)/shard_map/all_to_all | solution.py:183
  309.3 32.4 %reduce-scatter.2.cloned.1.call-done = f32[256,256]{1,0:T(8,128)} async-done(((f32[8192,256]{1,0:T(8,128)}), f32[256,256]{1,0:T(8,128)}) %reduce-scatter.2.cloned.1.call-update) | async-done | bytes 262160 | tf_op jit(solution)/shard_map/reduce_scatter | solution.py:168
  343.2 4.4 %all-to-all-start.6 = ((bf16[4,64,128]{2,1,0:T(8,128)(2,1)}), bf16[4,64,128]{2,1,0:T(8,128)(2,1)S(1)}, u32[]{:S(2)}, u32[]{:S(2)}) async-start(bf16[4,64,128]{2,1,0:T(8,128)(2,1)} %bitcast.61), calls=%async_computation.7 | async-start | bytes 131072 | tf_op jit(solution)/shard_map/all_to_all | solution.py:185
  349.2 4.1 %all-to-all-done.6 = bf16[4,64,128]{2,1,0:T(8,128)(2,1)S(1)} async-done(((bf16[4,64,128]{2,1,0:T(8,128)(2,1)}), bf16[4,64,128]{2,1,0:T(8,128)(2,1)S(1)}, u32[]{:S(2)}, u32[]{:S(2)}) %all-to-all-start.6) | async-done | bytes 65568 | tf_op jit(solution)/shard_map/all_to_all | solution.py:185
  357.2 5.0 %all-to-all-done.5 = bf16[4,64,128]{2,1,0:T(8,128)(2,1)S(1)} async-done(((bf16[4,64,128]{2,1,0:T(8,128)(2,1)}), bf16[4,64,128]{2,1,0:T(8,128)(2,1)S(1)}, u32[]{:S(2)}, u32[]{:S(2)}) %all-to-all-start.5) | async-done | bytes 65568 | tf_op jit(solution)/shard_map/all_to_all | solution.py:184
  (344 shorter events, 188.0 us)
Async XLA Ops:
  7.2 0.8 copy-start
  7.2 43.8 %copy-start.2 = (bf16[64,512]{1,0:T(8,128)(2,1)S(1)}, bf16[64,512]{1,0:T(8,128)(2,1)}, u32[]{:S(2)}) copy-start(bf16[64,512]{1,0:T(8,128)(2,1)} %param.19) | copy-start | bytes 196612
  7.2 49.2 %copy-start.3 = (bf16[64,512]{1,0:T(8,128)(2,1)S(1)}, bf16[64,512]{1,0:T(8,128)(2,1)}, u32[]{:S(2)}) copy-start(bf16[64,512]{1,0:T(8,128)(2,1)} %param.18) | copy-start | bytes 196612
  7.2 64.4 %all-gather.3.cloned.1.call-start = ((), (), s32[]{:S(2)}) async-start(), calls=%async_computation.8 | async-start | bytes 2162688 | tf_op jit(solution)/shard_map/all_gather | solution.py:79
  20.5 31.2 %all-to-all-start.1 = ((bf16[64,4,128]{2,0,1:T(8,128)(2,1)}), bf16[64,4,128]{2,0,1:T(8,128)(2,1)S(1)}, u32[]{:S(2)}, u32[]{:S(2)}) async-start(bf16[64,4,128]{2,0,1:T(8,128)(2,1)} %copy_bitcast_fusion.5), calls=%async_computation.1 | async-start | bytes 131072 | tf_op jit(solution)/shard_map/all_to_all | solution.py:63
  51.7 10.4 %all-to-all-start.3 = ((bf16[64,4,128]{2,0,1:T(8,128)(2,1)}), bf16[64,4,128]{2,0,1:T(8,128)(2,1)S(1)}, u32[]{:S(2)}, u32[]{:S(2)}) async-start(bf16[64,4,128]{2,0,1:T(8,128)(2,1)} %copy_bitcast_fusion.3), calls=%async_computation.3 | async-start | bytes 131072 | tf_op jit(solution)/shard_map/all_to_all | solution.py:66
  62.0 8.9 %all-to-all-start.2 = ((bf16[64,4,128]{2,0,1:T(8,128)(2,1)}), bf16[64,4,128]{2,0,1:T(8,128)(2,1)S(1)}, u32[]{:S(2)}, u32[]{:S(2)}) async-start(bf16[64,4,128]{2,0,1:T(8,128)(2,1)} %copy_bitcast_fusion.4), calls=%async_computation.2 | async-start | bytes 131072 | tf_op jit(solution)/shard_map/all_to_all | solution.py:65
  65.3 58.0 %all-gather.5.cloned.1.call-start = ((), (), s32[]{:S(2)}) async-start(), calls=%async_computation.9 | async-start | bytes 2162688 | tf_op jit(solution)/shard_map/all_gather | solution.py:80
  70.9 0.6 copy-start.1
  71.6 270.1 %reduce-scatter.2.cloned.1.call-start = ((), (), s32[]{:S(2)}) async-start(), calls=%async_computation.10 | async-start | bytes 8650752 | tf_op jit(solution)/shard_map/reduce_scatter | solution.py:168
  343.2 10.0 %all-to-all-start.6 = ((bf16[4,64,128]{2,1,0:T(8,128)(2,1)}), bf16[4,64,128]{2,1,0:T(8,128)(2,1)S(1)}, u32[]{:S(2)}, u32[]{:S(2)}) async-start(bf16[4,64,128]{2,1,0:T(8,128)(2,1)} %bitcast.61), calls=%async_computation.7 | async-start | bytes 131072 | tf_op jit(solution)/shard_map/all_to_all | solution.py:185
  353.2 8.9 %all-to-all-start.5 = ((bf16[4,64,128]{2,1,0:T(8,128)(2,1)}), bf16[4,64,128]{2,1,0:T(8,128)(2,1)S(1)}, u32[]{:S(2)}, u32[]{:S(2)}) async-start(bf16[4,64,128]{2,1,0:T(8,128)(2,1)} %bitcast.59), calls=%async_computation.6 | async-start | bytes 131072 | tf_op jit(solution)/shard_map/all_to_all | solution.py:184
Sparse Core Ops, SparseCore 0:
  19.1 43.2 all-gather.2
  71.7 43.1 all-gather.4
  249.5 92.0 reduce-scatter.1
where the time goes:
time: 371 us; the launch traced here: 369 us
  local copies, waits for them, and re-layouts  183 us (49%)
  waiting for transfers between devices  51.5 us (14%)
  other arithmetic  38.9 us (10%)
  matrix products  36.8 us (10%)
  starting transfers between devices  19.1 us (5%)
  blocking collectives  18.9 us (5%)
  between operations  14 us (4%)
  loops' own time  7.41 us (2%)
    gather x24, local copies, waits for them, and re-layouts, turn(): allowed = jnp.take(my_mask, key_tiles, axis=1) == 1  83.2 us
    reduce_scatter x1, waiting for transfers between devices, body(): lax.psum_scatter(lax.map(one_part, jnp.arange(amount // block_rows, dtype...  32.4 us
    gather x8, local copies, waits for them, and re-layouts, one_part(): allowed = jnp.take(my_mask, key_tiles, axis=1) == 1  27.7 us
    dynamic_slice x16, local copies, waits for them, and re-layouts, turn(): key_part = lax.dynamic_slice_in_dim(key_all, offset, block_rows, 0)  16.4 us
    add x1, other arithmetic, token_tiles(): return frames * (row_count // TILE) + places % row_count // TILE  15.9 us
    dot_general x24, matrix products, raw_scores(): jnp.einsum('qhd,khd->hqk', split_heads(query_part, local_heads), split_he...  13.4 us
    dynamic_update_slice x16, local copies, waits for them, and re-layouts, body(): lax.map(one_part, jnp.arange(amount // block_rows, dtype=jnp.int32))  11.2 us
    all_to_all x1, blocking collectives, body(): lax.all_to_all(keys, 'head', split_axis=1, concat_axis=0, tiled=True)  10.9 us
  transfers between devices with their start and end apart: 8, of which 5 were waited for; matrix products, arithmetic and copies ran while one was open for 37% of the time, Pallas kernels for 0%

commit v1 on v0

v1 whole, which is shorter than its diff:
```python
import functools

import jax
import jax.numpy as jnp
from jax import lax
from jax.experimental import pallas as pl
from jax.experimental.pallas import tpu as pltpu
from jax.sharding import PartitionSpec as P

HDIM = 64
TILE = 128
LANES = 128
HEADS = 8
ROWS = 64
TILES = 4
BLOCK = TILES * TILE
BLOCKS = 16
SLOTS = BLOCKS * TILES
GROUP = 4
PIECES = ((0, 176), (176, 176), (352, 160))
MESH = pl.DeviceIdType.MESH
F32 = jnp.float32
BF16 = jnp.bfloat16
BIG = 1e30
NT = (((1,), (1,)), ((), ()))
NN = (((1,), (0,)), ((), ()))
VMEM_SPEC = pl.BlockSpec(memory_space=pltpu.VMEM)
SMEM_SPEC = pl.BlockSpec(memory_space=pltpu.SMEM)


def here():
    blk = lax.axis_index("blk")
    z = lax.axis_index("head")
    return (blk // 8, (blk // 2) % 4, z), blk % 2


def device(place, core):
    x, y, z = place
    return ((x * 4 + y) * 2 + core, z)


def paired(v, flip):
    return v + (1 - 2 * (v % 2)) if flip else v


def half(v):
    return ((v + 1) // 2) % 2


def head_of(place, offset):
    bits = [(half(v) + d) % 2 for v, d in zip(place, offset)]
    return bits[0] * 4 + bits[1] * 2 + bits[2]


def block_of(place, core, offset=(0, 0, 0)):
    bits = [(v // 2 + d) % 2 for v, d in zip(place, offset)]
    return ((bits[0] * 2 + bits[1]) * 2 + bits[2]) * 2 + core


def entry_rows(place, offset=(0, 0, 0)):
    bits = [(v % 2 + d) % 2 for v, d in zip(place, offset)]
    return pl.multiple_of((bits[0] * 2 + bits[1]) * TILE + bits[2] * ROWS, ROWS)


OFFSETS = [(a, b, c) for a in (0, 1) for b in (0, 1) for c in (0, 1)][1:]


def pair_device(place, core, offset):
    return device([paired(v, d) for v, d in zip(place, offset)], core)


def mirror_device(place, core, axis):
    return device([3 - v if a == axis else v for a, v in enumerate(place)], core)


def remote(src, dst, send, recv, target):
    return pltpu.make_async_remote_copy(
        src_ref=src, dst_ref=dst, send_sem=send, recv_sem=recv, device_id=target, device_id_type=MESH
    )


def greet(targets):
    barrier = pltpu.get_barrier_semaphore()
    for target in targets:
        pl.semaphore_signal(barrier, inc=1, device_id=target, device_id_type=MESH)
    return lambda: pl.semaphore_wait(barrier, len(targets))


UNIT = [(1, 0, 0), (0, 1, 0), (0, 0, 1)]


def plus(*offsets):
    return tuple(sum(v) for v in zip(*offsets))


class CubeGather:
    def __init__(self, ref, place, core, send, recv, core_send, core_recv):
        self.ref, self.place, self.core = ref, place, core
        self.send, self.recv, self.core_send, self.core_recv = send, recv, core_send, core_recv

    def part(self, piece, offset, core=None):
        first, count = PIECES[piece]
        core = self.core if core is None else core
        return self.ref.at[block_of(self.place, core, offset), pl.ds(first, count), :]

    def hops(self, piece):
        a1, a2, a3 = [(piece + i) % 3 for i in range(3)]
        u1, u2, o = UNIT[a1], UNIT[a2], (0, 0, 0)
        return [(a1, o), (a2, o), (a2, u1), (a3, o), (a3, u1), (a3, u2), (a3, plus(u1, u2))]

    def out_copy(self, piece, k):
        axis, offset = self.hops(piece)[k]
        part = self.part(piece, offset)
        return remote(part, part, self.send.at[piece, k], self.recv.at[piece, k],
                      mirror_device(self.place, self.core, axis))

    def in_copy(self, piece, k):
        axis, offset = self.hops(piece)[k]
        part = self.part(piece, plus(offset, UNIT[axis]))
        return remote(part, part, self.send.at[piece, k], self.recv.at[piece, k],
                      mirror_device(self.place, self.core, axis))

    def core_copy(self, piece, k, core=None):
        if k == 7:
            offset = (0, 0, 0)
        else:
            axis, offset = self.hops(piece)[k]
            offset = plus(offset, UNIT[axis])
        part = self.part(piece, offset, core)
        return remote(part, part, self.core_send.at[piece, k], self.core_recv.at[piece, k],
                      device(self.place, 1 - self.core))

    def begin(self):
        for k in (0, 1, 3):
            for p in range(3):
                self.out_copy(p, k).start()
        for p in range(3):
            self.core_copy(p, 7).start()

    def relay(self):
        for k, onward in ((0, (2, 4)), (1, (5,)), (2, (6,)), (3, ()), (4, ()), (5, ()), (6, ())):
            for p in range(3):
                self.in_copy(p, k).wait_recv()
                for j in onward:
                    self.out_copy(p, j).start()
                self.core_copy(p, k).start()

    def finish(self):
        for k in (7, 0, 1, 2, 3, 4, 5, 6):
            for p in range(3):
                self.core_copy(p, k, 1 - self.core).wait_recv()
        for p in range(3):
            for k in range(7):
                self.out_copy(p, k).wait_send()
            for k in range(8):
                self.core_copy(p, k).wait_send()


GATHER_SEMS = [
    pltpu.SemaphoreType.DMA((3, 7)),
    pltpu.SemaphoreType.DMA((3, 7)),
    pltpu.SemaphoreType.DMA((3, 8)),
    pltpu.SemaphoreType.DMA((3, 8)),
]


def low_lanes(rows):
    return lax.broadcasted_iota(jnp.int32, (rows, LANES), 1) < HDIM


def pack_heads(first_ref, second_ref, packed, scale=None):
    low = low_lanes(ROWS)
    for j in range(HEADS // 2):
        columns = slice(j * LANES, (j + 1) * LANES)
        one = first_ref[:, columns].astype(F32)
        two = second_ref[:, columns].astype(F32)
        if scale is not None:
            one = one * scale
        packed[2 * j] = jnp.where(low, one, pltpu.roll(two, HDIM, 1)).astype(BF16)
        packed[2 * j + 1] = jnp.where(low, pltpu.roll(one, HDIM, 1), two).astype(BF16)


def enter_kernel(q_ref, k_ref, v_ref, g_ref, kv_ref, kv_own, qg_own, kv_pack, qg_pack,
                 pair_send, pair_recv, send, recv, core_send, core_recv):
    place, core = here()
    wait_all = greet(
        [pair_device(place, core, o) for o in OFFSETS]
        + [mirror_device(place, core, a) for a in range(3)]
        + [device(place, 1 - core)]
    )
    own = block_of(place, core)
    mine = entry_rows(place)

    def pair_copy(which, i):
        packed = (kv_pack, qg_pack)[which]
        landing = kv_ref.at[own, pl.ds(mine, ROWS), :] if which == 0 else qg_own.at[pl.ds(mine, ROWS), :]
        return remote(packed.at[head_of(place, OFFSETS[i])], landing, pair_send.at[which, i],
                      pair_recv.at[which, i], pair_device(place, core, OFFSETS[i]))

    def pair_arrival(which, i):
        rows = entry_rows(place, OFFSETS[i])
        landing = kv_ref.at[own, pl.ds(rows, ROWS), :] if which == 0 else qg_own.at[pl.ds(rows, ROWS), :]
        packed = (kv_pack, qg_pack)[which]
        return remote(packed.at[head_of(place, OFFSETS[i])], landing, pair_send.at[which, i],
                      pair_recv.at[which, i], pair_device(place, core, OFFSETS[i]))

    pack_heads(k_ref, v_ref, kv_pack)
    wait_all()
    for i in range(7):
        pair_copy(0, i).start()
    kv_ref[own, pl.ds(mine, ROWS), :] = kv_pack[head_of(place, (0, 0, 0))]
    pack_heads(q_ref, g_ref, qg_pack, HDIM ** -0.5)
    for i in range(7):
        pair_copy(1, i).start()
    qg_own[pl.ds(mine, ROWS), :] = qg_pack[head_of(place, (0, 0, 0))]
    for i in range(7):
        pair_arrival(0, i).wait_recv()
    gather = CubeGather(kv_ref, place, core, send, recv, core_send, core_recv)
    gather.begin()
    kv_own[...] = kv_ref[own]
    gather.relay()
    for i in range(7):
        pair_arrival(1, i).wait_recv()
    for which in range(2):
        for i in range(7):
            pair_copy(which, i).wait_send()
    gather.finish()


def enter(q, k, v, g):
    return pl.pallas_call(
        enter_kernel,
        name="enter",
        out_shape=(
            jax.ShapeDtypeStruct((BLOCKS, BLOCK, LANES), BF16),
            jax.ShapeDtypeStruct((BLOCK, LANES), BF16),
            jax.ShapeDtypeStruct((BLOCK, LANES), BF16),
        ),
        in_specs=[VMEM_SPEC] * 4,
        out_specs=(VMEM_SPEC,) * 3,
        scratch_shapes=[
            pltpu.VMEM((HEADS, ROWS, LANES), BF16),
            pltpu.VMEM((HEADS, ROWS, LANES), BF16),
            pltpu.SemaphoreType.DMA((2, 7)),
            pltpu.SemaphoreType.DMA((2, 7)),
        ] + GATHER_SEMS,
        compiler_params=pltpu.CompilerParams(
            collective_id=0, has_side_effects=True, vmem_limit_bytes=16 * 2**20
        ),
    )(q, k, v, g)


def share_kernel(qg_own, stat_own, qg_ref, stat_ref, stat_send, stat_recv, send, recv, core_send, core_recv):
    place, core = here()
    peers = [(o, c) for o in [(0, 0, 0)] + OFFSETS for c in (0, 1)][1:]

    def peer_device(offset, flip):
        mirrored = [3 - v if d else v for v, d in zip(place, offset)]
        return device(mirrored, (core + flip) % 2)

    wait_all = greet([peer_device(*p) for p in peers])
    own = block_of(place, core)
    qg_ref[own] = qg_own[...]
    stat_ref[own] = stat_own[...]
    wait_all()
    gather = CubeGather(qg_ref, place, core, send, recv, core_send, core_recv)

    def stat_copy(i):
        part = stat_ref.at[own]
        return remote(part, part, stat_send.at[i], stat_recv.at[i], peer_device(*peers[i]))

    def stat_arrival(i):
        offset, flip = peers[i]
        part = stat_ref.at[block_of(place, (core + flip) % 2, offset)]
        return remote(part, part, stat_send.at[i], stat_recv.at[i], peer_device(*peers[i]))

    gather.begin()
    for i in range(15):
        stat_copy(i).start()
    gather.relay()
    for i in range(15):
        stat_arrival(i).wait_recv()
    for i in range(15):
        stat_copy(i).wait_send()
    gather.finish()


def share(qg_own, stat_own):
    return pl.pallas_call(
        share_kernel,
        name="share",
        out_shape=(
            jax.ShapeDtypeStruct((BLOCKS, BLOCK, LANES), BF16),
            jax.ShapeDtypeStruct((BLOCKS, 8, LANES), F32),
        ),
        in_specs=[VMEM_SPEC] * 2,
        out_specs=(VMEM_SPEC,) * 2,
        scratch_shapes=[pltpu.SemaphoreType.DMA((15,)), pltpu.SemaphoreType.DMA((15,))] + GATHER_SEMS,
        compiler_params=pltpu.CompilerParams(
            collective_id=1, has_side_effects=True, vmem_limit_bytes=16 * 2**20
        ),
    )(qg_own, stat_own)


def fill_table(order_ref, table):
    for slot in range(SLOTS):
        b, t = slot // TILES, slot % TILES
        x = 2 * (b // 8) + t // 2
        y = 2 * ((b // 4) % 2) + t % 2
        table[slot] = order_ref[(x * 4 + y) * 2 + b % 2] * 2 + (b // 2) % 2


def fill_list(allowed, listed):
    count = jnp.int32(0)
    for slot in range(SLOTS):
        listed[count] = slot
        count = count + allowed(slot)
    first = listed[0]
    for i in range(GROUP - 1):
        listed[count + i] = first
    return count


def query_kernel(kv_ref, qg_own, mask_ref, order_ref, stat_ref, dq_ref, table, listed, score_buf, stat_buf):
    place, core = here()
    own = block_of(place, core)
    fill_table(order_ref, table)
    low = low_lanes(TILE)
    lane = lax.broadcasted_iota(jnp.int32, (TILE, LANES), 1)
    zero = jnp.zeros((TILE, LANES), BF16)
    zeros = jnp.zeros((TILE, LANES), F32)

    def one_tile(t, unused):
        tile = table[own * TILES + t]
        count = fill_list(lambda s: (mask_ref[tile, table[s]] == 1).astype(jnp.int32), listed)
        steps = (count + GROUP - 1) // GROUP
        both = qg_own[t]
        query = jnp.where(low, both, zero)
        grad = jnp.where(low, zero, both)

        def keys_of(step):
            return jnp.concatenate([kv_ref[listed[step * GROUP + u]] for u in range(GROUP)], axis=0)

        def cut(wide, u):
            return wide[:, u * TILE : (u + 1) * TILE]

        def scores_step(step, peak):
            scores = lax.dot_general(query, keys_of(step), NT, preferred_element_type=F32)
            score_buf[step] = scores
            for u in range(GROUP):
                peak = jnp.maximum(peak, cut(scores, u))
            return peak

        peak = lax.fori_loop(0, steps, scores_step, jnp.full((TILE, LANES), -BIG, F32))
        peak = jnp.max(peak, axis=1, keepdims=True)

        def exp_step(step, mass):
            for u in range(GROUP):
                less = jnp.where(step * GROUP + u < count, 0.0, BIG).astype(F32)
                columns = slice(u * TILE, (u + 1) * TILE)
                term = jnp.exp(score_buf[step, :, columns] - (peak + less))
                score_buf[step, :, columns] = term
                mass = mass + term
            return mass

        mass = lax.fori_loop(0, steps, exp_step, zeros)
        mass = jnp.sum(mass, axis=1, keepdims=True)
        inverse = 1.0 / mass
        log_mass = peak + jnp.log(mass)

        def out_step(step, out):
            probs = (score_buf[step] * inverse).astype(BF16)
            return out + lax.dot_general(probs, keys_of(step), NN, preferred_element_type=F32)

        out = lax.fori_loop(0, steps, out_step, zeros)
        out = out.astype(BF16).astype(F32)
        delta = jnp.sum(jnp.where(low, 0.0, both.astype(F32) * out), axis=1, keepdims=True)

        def grad_step(step, acc):
            keys = keys_of(step)
            prob_grad = lax.dot_general(grad, keys, NT, preferred_element_type=F32)
            score_grad = ((score_buf[step] * inverse) * (prob_grad - delta)).astype(BF16)
            return acc + lax.dot_general(score_grad, keys, NN, preferred_element_type=F32)

        acc = lax.fori_loop(0, steps, grad_step, zeros) * HDIM ** -0.5
        low_part = low_lanes(ROWS // 2)
        for i in range(2):
            top = acc[i * ROWS : i * ROWS + ROWS // 2]
            bottom = acc[i * ROWS + ROWS // 2 : (i + 1) * ROWS]
            dq_ref[2 * t + i] = jnp.where(low_part, top, pltpu.roll(bottom, HDIM, 1)).astype(BF16)
        stats = jnp.where(lane == t, log_mass, stat_buf[...])
        stat_buf[...] = jnp.where(lane == TILES + t, delta, stats)
        return unused

    stat_buf[...] = zeros
    lax.fori_loop(0, TILES, one_tile, 0)
    stat_ref[...] = stat_buf[...].T[:8]


def query_side(kv, qg_own, tile_mask, frame_order):
    return pl.pallas_call(
        query_kernel,
        name="query_side",
        out_shape=(
            jax.ShapeDtypeStruct((8, LANES), F32),
            jax.ShapeDtypeStruct((2 * TILES, ROWS // 2, LANES), BF16),
        ),
        in_specs=[VMEM_SPEC, VMEM_SPEC, SMEM_SPEC, SMEM_SPEC],
        out_specs=(VMEM_SPEC,) * 2,
        scratch_shapes=[
            pltpu.SMEM((SLOTS,), jnp.int32),
            pltpu.SMEM((SLOTS + GROUP,), jnp.int32),
            pltpu.VMEM((SLOTS // GROUP, TILE, GROUP * TILE), F32),
            pltpu.VMEM((TILE, LANES), F32),
        ],
        compiler_params=pltpu.CompilerParams(vmem_limit_bytes=24 * 2**20),
    )(kv.reshape(SLOTS, TILE, LANES), qg_own.reshape(TILES, TILE, LANES), tile_mask, frame_order)


def key_kernel(qg_ref, stat_ref, kv_own, mask_ref, order_ref, dkv_ref, table, listed, rows_ref):
    place, core = here()
    own = block_of(place, core)
    fill_table(order_ref, table)
    for b in range(BLOCKS):
        for t in range(TILES):
            rows_ref[b * TILES + t, 0:1, :] = stat_ref[b, t : t + 1, :]
            rows_ref[b * TILES + t, 1:2, :] = stat_ref[b, TILES + t : TILES + t + 1, :]
    low = low_lanes(TILE)
    zero = jnp.zeros((TILE, LANES), BF16)

    def one_tile(t, unused):
        tile = table[own * TILES + t]
        count = fill_list(lambda s: (mask_ref[table[s], tile] == 1).astype(jnp.int32), listed)
        steps = (count + GROUP - 1) // GROUP
        both = kv_own[t]
        stacked = jnp.concatenate([jnp.where(low, both, zero), jnp.where(low, zero, both)], axis=0)

        def step_terms(step, acc):
            lefts, rights = [], []
            for u in range(GROUP):
                slot = listed[step * GROUP + u]
                less = jnp.where(step * GROUP + u < count, 0.0, BIG).astype(F32)
                queries = qg_ref[slot]
                products = lax.dot_general(stacked, queries, NT, preferred_element_type=F32)
                probs = jnp.exp(products[:TILE] - (rows_ref[slot, 0:1, :] + less))
                score_grad = probs * (products[TILE:] - rows_ref[slot, 1:2, :])
                lefts += [score_grad.astype(BF16), probs.astype(BF16)]
                rights += [jnp.where(low, queries, zero), jnp.where(low, zero, queries)]
            return acc + lax.dot_general(
                jnp.concatenate(lefts, axis=1), jnp.concatenate(rights, axis=0), NN,
                preferred_element_type=F32,
            )

        acc = lax.fori_loop(0, steps, step_terms, jnp.zeros((TILE, LANES), F32))
        dkv_ref[t] = acc.astype(BF16)
        return unused

    lax.fori_loop(0, TILES, one_tile, 0)


def key_side(qg, stats, kv_own, tile_mask, frame_order):
    return pl.pallas_call(
        key_kernel,
        name="key_side",
        out_shape=jax.ShapeDtypeStruct((TILES, TILE, LANES), BF16),
        in_specs=[VMEM_SPEC, VMEM_SPEC, VMEM_SPEC, SMEM_SPEC, SMEM_SPEC],
        out_specs=VMEM_SPEC,
        scratch_shapes=[
            pltpu.SMEM((SLOTS,), jnp.int32),
            pltpu.SMEM((SLOTS + GROUP,), jnp.int32),
            pltpu.VMEM((SLOTS, 8, LANES), F32),
        ],
        compiler_params=pltpu.CompilerParams(vmem_limit_bytes=24 * 2**20),
    )(qg.reshape(SLOTS, TILE, LANES), stats, kv_own.reshape(TILES, TILE, LANES), tile_mask, frame_order)


def leave_kernel(dq_ref, dkv_ref, q_out, k_out, v_out, dq_got, dkv_got, pair_send, pair_recv):
    place, core = here()
    wait_all = greet([pair_device(place, core, o) for o in OFFSETS])
    mine = head_of(place, (0, 0, 0))
    sources, landings = (dq_ref, dkv_ref), (dq_got, dkv_got)

    def share_of(offset):
        bits = [(v % 2 + d) % 2 for v, d in zip(place, offset)]
        return (bits[0] * 2 + bits[1]) * 2 + bits[2]

    def pair_copy(which, i):
        return remote(sources[which].at[share_of(OFFSETS[i])], landings[which].at[mine],
                      pair_send.at[which, i], pair_recv.at[which, i], pair_device(place, core, OFFSETS[i]))

    def pair_arrival(which, i):
        return remote(sources[which].at[share_of(OFFSETS[i])], landings[which].at[head_of(place, OFFSETS[i])],
                      pair_send.at[which, i], pair_recv.at[which, i], pair_device(place, core, OFFSETS[i]))

    wait_all()
    for which in (1, 0):
        for i in range(7):
            pair_copy(which, i).start()
    dq_got[mine] = dq_ref[share_of((0, 0, 0))]
    dkv_got[mine] = dkv_ref[share_of((0, 0, 0))]
    for i in range(7):
        pair_arrival(1, i).wait_recv()
    low = low_lanes(ROWS)
    for j in range(HEADS // 2):
        columns = slice(j * LANES, (j + 1) * LANES)
        one = dkv_got[2 * j].astype(F32)
        two = dkv_got[2 * j + 1].astype(F32)
        k_out[:, columns] = jnp.where(low, one, pltpu.roll(two, HDIM, 1)).astype(BF16)
        v_out[:, columns] = jnp.where(low, pltpu.roll(one, HDIM, 1), two).astype(BF16)
    for i in range(7):
        pair_arrival(0, i).wait_recv()
    low = low_lanes(ROWS // 2)
    for j in range(HEADS // 2):
        columns = slice(j * LANES, (j + 1) * LANES)
        one = dq_got[2 * j].astype(F32)
        two = dq_got[2 * j + 1].astype(F32)
        q_out[0 : ROWS // 2, columns] = jnp.where(low, one, pltpu.roll(two, HDIM, 1)).astype(BF16)
        q_out[ROWS // 2 : ROWS, columns] = jnp.where(low, pltpu.roll(one, HDIM, 1), two).astype(BF16)
    for which in (1, 0):
        for i in range(7):
            pair_copy(which, i).wait_send()


def leave(dq, dkv):
    return pl.pallas_call(
        leave_kernel,
        name="leave",
        out_shape=(jax.ShapeDtypeStruct((ROWS, HEADS * HDIM), BF16),) * 3,
        in_specs=[VMEM_SPEC] * 2,
        out_specs=(VMEM_SPEC,) * 3,
        scratch_shapes=[
            pltpu.VMEM((HEADS, ROWS // 2, LANES), BF16),
            pltpu.VMEM((HEADS, ROWS, LANES), BF16),
            pltpu.SemaphoreType.DMA((2, 7)),
            pltpu.SemaphoreType.DMA((2, 7)),
        ],
        compiler_params=pltpu.CompilerParams(
            collective_id=2, has_side_effects=True, vmem_limit_bytes=8 * 2**20
        ),
    )(dq, dkv.reshape(HEADS, ROWS, LANES))


def body(queries, keys, values, out_grad, tile_mask, frame_order):
    kv, kv_own, qg_own = enter(queries, keys, values, out_grad)
    stats_own, dq = query_side(kv, qg_own, tile_mask, frame_order)
    qg, stats = share(qg_own, stats_own)
    dkv = key_side(qg, stats, kv_own, tile_mask, frame_order)
    return leave(dq, dkv)


def solution(mesh):
    whole = P(("blk", "head"), None)
    return jax.shard_map(
        body,
        mesh=mesh,
        in_specs=(whole,) * 4 + (P(), P()),
        out_specs=(whole,) * 3,
        check_vma=False,
    )
```

time: 371 us -> 85.3 us (0.23)
  local copies, waits for them, and re-layouts: 183 us -> 6.66 us
  Pallas kernels: 0 us -> 76.3 us
  waiting for transfers between devices: 51.5 us -> 0 us
  other arithmetic: 38.9 us -> 0 us
  matrix products: 36.8 us -> 0 us
  starting transfers between devices: 19.1 us -> 0 us
  blocking collectives: 18.9 us -> 0 us
  between operations: 14 us -> 0.71 us
  loops' own time: 7.41 us -> 0 us
    gather x35 -> x0, local copies, waits for them, and re-layouts: 116 us -> none  [the longest x24 83.2 us: turn(): allowed = jnp.take(my_mask, key_tiles, axis=1) == 1]
    pallas_call x0 -> x5, Pallas kernels: none -> 76.3 us  [the longest x1 25.1 us: enter(): pl.pallas_call(enter_kernel, name='enter', out_shape=(jax.ShapeDtypeStruc...]
    dynamic_slice x40 -> x0, local copies, waits for them, and re-layouts: 38.4 us -> none  [the longest x16 16.4 us: turn(): key_part = lax.dynamic_slice_in_dim(key_all, offset, block_rows, 0)]
    dot_general x56 -> x0, matrix products: 36.8 us -> none  [the longest x24 13.4 us: raw_scores(): jnp.einsum('qhd,khd->hqk', split_heads(query_part, local_heads), split_he...]
    reduce_scatter x1 -> x0, waiting for transfers between devices: 32.4 us -> none  [body(): lax.psum_scatter(lax.map(one_part, jnp.arange(amount // block_rows, dtype...]
    all_to_all x5 -> x0, waiting for transfers between devices: 19 us -> none  [the longest x1 5.1 us: body(): lax.all_to_all(values, 'head', split_axis=1, concat_axis=0, tiled=True)]
    all_to_all x5 -> x0, starting transfers between devices: 19 us -> none  [the longest x1 4.74 us: body(): lax.all_to_all(out_grad, 'head', split_axis=1, concat_axis=0, tiled=True)]
    all_to_all x2 -> x0, blocking collectives: 18.9 us -> none  [the longest x1 10.9 us: body(): lax.all_to_all(keys, 'head', split_axis=1, concat_axis=0, tiled=True)]
  transfers between devices with their start and end apart: 8 -> 0, of which waited for: 5 -> 0; matrix products, arithmetic and copies ran while one was open for 37% -> 0% of each run, Pallas kernels for 0% -> 0%
where the time goes in v1:
time: 85.3 us; the launch traced here: 83.7 us
  Pallas kernels  76.3 us (89%)
  local copies, waits for them, and re-layouts  6.66 us (8%)
    pallas_call x1, Pallas kernels, enter(): pl.pallas_call(enter_kernel, name='enter', out_shape=(jax.ShapeDtypeStruc...  25.1 us
    pallas_call x1, Pallas kernels, share(): pl.pallas_call(share_kernel, name='share', out_shape=(jax.ShapeDtypeStruc...  20.6 us
    pallas_call x1, Pallas kernels, query_side(): pl.pallas_call(query_kernel, name='query_side', out_shape=(jax.ShapeDtype...  15.6 us
    pallas_call x1, Pallas kernels, leave(): pl.pallas_call(leave_kernel, name='leave', out_shape=(jax.ShapeDtypeStruc...  7.83 us
    pallas_call x1, Pallas kernels, key_side(): pl.pallas_call(key_kernel, name='key_side', out_shape=jax.ShapeDtypeStruc...  7.2 us
    unnamed x19, local copies, waits for them, and re-layouts  6.66 us

profile of v1, /device:TPU:0, one launch (start us, length us, event | category | flops | bytes accessed | tf_op | source)
XLA Modules:
  0.0 83.7 jit_solution(1210178415437280255)
XLA Ops:
  0.6 0.0 copy-start.1
  0.6 0.0 copy-start.2
  0.7 0.8 copy-done.2
  1.5 0.0 copy-start.3
  1.5 0.8 %copy-done.3 = bf16[64,512]{1,0:T(8,128)(2,1)S(1)} copy-done((bf16[64,512]{1,0:T(8,128)(2,1)S(1)}, bf16[64,512]{1,0:T(8,128)(2,1)}, u32[]{:S(2)}) %copy-start.3) | copy-done | bytes 65560
  2.3 0.0 copy-start.4
  2.3 0.8 %copy-done.4 = bf16[64,512]{1,0:T(8,128)(2,1)S(1)} copy-done((bf16[64,512]{1,0:T(8,128)(2,1)S(1)}, bf16[64,512]{1,0:T(8,128)(2,1)}, u32[]{:S(2)}) %copy-start.4) | copy-done | bytes 65560
  3.2 0.0 copy-start.5
  3.2 0.8 %copy-done.5 = bf16[64,512]{1,0:T(8,128)(2,1)S(1)} copy-done((bf16[64,512]{1,0:T(8,128)(2,1)S(1)}, bf16[64,512]{1,0:T(8,128)(2,1)}, u32[]{:S(2)}) %copy-start.5) | copy-done | bytes 65560
  4.0 0.0 copy-start.7
  4.0 25.1 %enter.1 = (bf16[16,512,128]{2,1,0:T(8,128)(2,1)S(1)}, bf16[512,128]{1,0:T(8,128)(2,1)S(1)}, bf16[512,128]{1,0:T(8,128)(2,1)S(1)}) custom-call(bf16[64,512]{1,0:T(8,128)(2,1)S(1)} %copy-done.2, bf16[64,512]{1,0:T(8,128)(2,1)S(1)} %copy-done.3, bf16[64,512]{1,0:T(8,128)(2,1)S(1)} %copy-done.4, bf16[64,512]{1,0:T(8,128)(2,1)S(1)} %copy-done.5), custom_call_target="tpu_custom_call" | custom-call | tf_op jit(solution)/shard_map/enter/pallas_call | solution.py:231
  29.1 0.0 copy-start
  29.1 0.7 copy-done
  29.8 0.0 copy-start.6
  29.9 0.7 copy-done.6
  30.5 15.6 %query_side.1 = (f32[8,128]{1,0:T(8,128)S(1)}, bf16[8,32,128]{2,1,0:T(8,128)(2,1)S(1)}) custom-call(bf16[64,128,128]{2,1,0:T(8,128)(2,1)S(1)} %bitcast.5, bf16[4,128,128]{2,1,0:T(8,128)(2,1)S(1)} %bitcast.7, s32[64,64]{1,0:T(8,128)S(1)} %copy-done, s32[32]{0:T(128)S(1)} %copy-done.6), custom_call_target="tpu_custom_call" | custom-call | tf_op jit(solution)/shard_map/query_side/pallas_call | solution.py:401
  46.1 20.6 %share.1 = (bf16[16,512,128]{2,1,0:T(8,128)(2,1)S(1)}, f32[16,8,128]{2,1,0:T(8,128)S(1)}) custom-call(bf16[512,128]{1,0:T(8,128)(2,1)S(1)} %get-tuple-element.11.qg_own, f32[8,128]{1,0:T(8,128)S(1)} %get-tuple-element.13.stat_own), custom_call_target="tpu_custom_call" | custom-call | tf_op jit(solution)/shard_map/share/pallas_call | solution.py:289
  66.7 0.0 copy-done.1
  66.7 0.0 copy-done.7
  66.8 7.2 %key_side.1 = bf16[4,128,128]{2,1,0:T(8,128)(2,1)S(1)} custom-call(bf16[64,128,128]{2,1,0:T(8,128)(2,1)S(1)} %bitcast.6, f32[16,8,128]{2,1,0:T(8,128)S(1)} %get-tuple-element.15.stat_ref, bf16[4,128,128]{2,1,0:T(8,128)(2,1)S(1)} %bitcast.9, s32[64,64]{1,0:T(8,128)S(1)} %copy-done.1, s32[32]{0:T(128)S(1)} %copy-done.7), custom_call_target="tpu_custom_call" | custom-call | tf_op jit(solution)/shard_map/key_side/pallas_call | solution.py:462
  74.0 7.8 %leave.1 = (bf16[64,512]{1,0:T(8,128)(2,1)S(1)}, bf16[64,512]{1,0:T(8,128)(2,1)S(1)}, bf16[64,512]{1,0:T(8,128)(2,1)S(1)}) custom-call(bf16[8,32,128]{2,1,0:T(8,128)(2,1)S(1)} %get-tuple-element.12.dq_ref, bf16[8,64,128]{2,1,0:T(8,128)(2,1)S(1)} %bitcast.8), custom_call_target="tpu_custom_call" | custom-call | tf_op jit(solution)/shard_map/leave/pallas_call | solution.py:525
  81.8 0.6 copy.12
  82.4 0.6 copy.13
  83.1 0.6 copy.14
Async XLA Ops:
  0.6 66.1 %copy-start.1 = (s32[64,64]{1,0:T(8,128)S(1)}, s32[64,64]{1,0:T(8,128)}, u32[]{:S(2)}) copy-start(s32[64,64]{1,0:T(8,128)} %mask_ref.3) | copy-start | bytes 49156
  0.6 0.8 %copy-start.2 = (bf16[64,512]{1,0:T(8,128)(2,1)S(1)}, bf16[64,512]{1,0:T(8,128)(2,1)}, u32[]{:S(2)}) copy-start(bf16[64,512]{1,0:T(8,128)(2,1)} %q_ref.1) | copy-start | bytes 196612
  1.5 0.8 %copy-start.3 = (bf16[64,512]{1,0:T(8,128)(2,1)S(1)}, bf16[64,512]{1,0:T(8,128)(2,1)}, u32[]{:S(2)}) copy-start(bf16[64,512]{1,0:T(8,128)(2,1)} %k_ref.1) | copy-start | bytes 196612
  2.3 0.8 %copy-start.4 = (bf16[64,512]{1,0:T(8,128)(2,1)S(1)}, bf16[64,512]{1,0:T(8,128)(2,1)}, u32[]{:S(2)}) copy-start(bf16[64,512]{1,0:T(8,128)(2,1)} %v_ref.1) | copy-start | bytes 196612
  3.2 0.8 %copy-start.5 = (bf16[64,512]{1,0:T(8,128)(2,1)S(1)}, bf16[64,512]{1,0:T(8,128)(2,1)}, u32[]{:S(2)}) copy-start(bf16[64,512]{1,0:T(8,128)(2,1)} %g_ref.1) | copy-start | bytes 196612
  4.0 62.7 %copy-start.7 = (s32[32]{0:T(128)S(1)}, s32[32]{0:T(128)}, u32[]{:S(2)}) copy-start(s32[32]{0:T(128)} %order_ref.3) | copy-start | bytes 388
  29.1 0.8 copy-start
  29.8 0.7 copy-start.6

commit v2 on v1

v2 whole, which is shorter than its diff:
```python
import functools

import jax
import jax.numpy as jnp
from jax import lax
from jax.experimental import pallas as pl
from jax.experimental.pallas import tpu as pltpu
from jax.sharding import PartitionSpec as P

HDIM = 64
TILE = 128
LANES = 128
HEADS = 8
ROWS = 64
TILES = 4
BLOCK = TILES * TILE
BLOCKS = 16
SLOTS = BLOCKS * TILES
GROUP = 8
PIECES = ((0, 176), (176, 176), (352, 160))
MESH = pl.DeviceIdType.MESH
F32 = jnp.float32
BF16 = jnp.bfloat16
BIG = 1e30
NT = (((1,), (1,)), ((), ()))
NN = (((1,), (0,)), ((), ()))
HBM_SPEC = pl.BlockSpec(memory_space=pltpu.HBM)
VMEM_SPEC = pl.BlockSpec(memory_space=pltpu.VMEM)
SMEM_SPEC = pl.BlockSpec(memory_space=pltpu.SMEM)


def here():
    blk = lax.axis_index("blk")
    z = lax.axis_index("head")
    return (blk // 8, (blk // 2) % 4, z), blk % 2


def device(place, core):
    x, y, z = place
    return ((x * 4 + y) * 2 + core, z)


def paired(v, flip):
    return v + (1 - 2 * (v % 2)) if flip else v


def half(v):
    return ((v + 1) // 2) % 2


def head_of(place, offset):
    bits = [(half(v) + d) % 2 for v, d in zip(place, offset)]
    return bits[0] * 4 + bits[1] * 2 + bits[2]


def block_of(place, core, offset=(0, 0, 0)):
    bits = [(v // 2 + d) % 2 for v, d in zip(place, offset)]
    return ((bits[0] * 2 + bits[1]) * 2 + bits[2]) * 2 + core


def entry_rows(place, offset=(0, 0, 0)):
    bits = [(v % 2 + d) % 2 for v, d in zip(place, offset)]
    return pl.multiple_of((bits[0] * 2 + bits[1]) * TILE + bits[2] * ROWS, ROWS)


ALL_OFFSETS = [(a, b, c) for a in (0, 1) for b in (0, 1) for c in (0, 1)]
OFFSETS = ALL_OFFSETS[1:]


def pair_device(place, core, offset):
    return device([paired(v, d) for v, d in zip(place, offset)], core)


def mirror_device(place, core, axis):
    return device([3 - v if a == axis else v for a, v in enumerate(place)], core)


def remote(src, dst, send, recv, target):
    return pltpu.make_async_remote_copy(
        src_ref=src, dst_ref=dst, send_sem=send, recv_sem=recv, device_id=target, device_id_type=MESH
    )


def greet(targets):
    barrier = pltpu.get_barrier_semaphore()
    for target in targets:
        pl.semaphore_signal(barrier, inc=1, device_id=target, device_id_type=MESH)
    return lambda: pl.semaphore_wait(barrier, len(targets))


UNIT = [(1, 0, 0), (0, 1, 0), (0, 0, 1)]


def plus(*offsets):
    return tuple(sum(v) for v in zip(*offsets))


class CubeGather:
    def __init__(self, ref, place, core, sems):
        self.ref, self.place, self.core = ref, place, core
        self.send, self.recv, self.core_send, self.core_recv = sems
        self.pieces = [0] * len(ALL_OFFSETS)

    def hops(self, piece):
        a1, a2, a3 = [(piece + i) % 3 for i in range(3)]
        u1, u2, o = UNIT[a1], UNIT[a2], (0, 0, 0)
        return [(a1, o), (a2, o), (a2, u1), (a3, o), (a3, u1), (a3, u2), (a3, plus(u1, u2))]

    def hop_copy(self, piece, k, arriving=False):
        axis, offset = self.hops(piece)[k]
        if arriving:
            offset = plus(offset, UNIT[axis])
        first, count = PIECES[piece]
        part = self.ref.at[block_of(self.place, self.core, offset), pl.ds(first, count), :]
        return remote(part, part, self.send.at[piece, k], self.recv.at[piece, k],
                      mirror_device(self.place, self.core, axis))

    def core_copy(self, i, arriving=False):
        core = 1 - self.core if arriving else self.core
        part = self.ref.at[block_of(self.place, core, ALL_OFFSETS[i])]
        return remote(part, part, self.core_send.at[i], self.core_recv.at[i],
                      device(self.place, 1 - self.core))

    def begin(self):
        for k in (0, 1, 3):
            for p in range(3):
                self.hop_copy(p, k).start()
        self.core_copy(0).start()

    def relay_step(self, k, onward):
        for p in range(3):
            self.hop_copy(p, k, True).wait_recv()
            for j in onward:
                self.hop_copy(p, j).start()
            axis, offset = self.hops(p)[k]
            i = ALL_OFFSETS.index(plus(offset, UNIT[axis]))
            self.pieces[i] += 1
            if self.pieces[i] == 3:
                self.core_copy(i).start()

    def finish(self):
        for i in range(8):
            self.core_copy(i, True).wait_recv()
        for p in range(3):
            for k in range(7):
                self.hop_copy(p, k).wait_send()
        for i in range(8):
            self.core_copy(i).wait_send()


GATHER_SEMS = [
    pltpu.SemaphoreType.DMA((3, 7)),
    pltpu.SemaphoreType.DMA((3, 7)),
    pltpu.SemaphoreType.DMA((8,)),
    pltpu.SemaphoreType.DMA((8,)),
]


def low_lanes(rows):
    return lax.broadcasted_iota(jnp.int32, (rows, LANES), 1) < HDIM


def pack_heads(first_ref, second_ref, packed, scale=None):
    low = low_lanes(ROWS)
    for j in range(HEADS // 2):
        columns = slice(j * LANES, (j + 1) * LANES)
        one = first_ref[:, columns].astype(F32)
        two = second_ref[:, columns].astype(F32)
        if scale is not None:
            one = one * scale
        packed[2 * j] = jnp.where(low, one, pltpu.roll(two, HDIM, 1)).astype(BF16)
        packed[2 * j + 1] = jnp.where(low, pltpu.roll(one, HDIM, 1), two).astype(BF16)


def slot_lists(mask, order, place, core):
    def dot(a, b, dims=NN):
        return lax.dot_general(a.astype(BF16), b.astype(BF16), dims, preferred_element_type=F32)

    def iota(shape, dim):
        return lax.broadcasted_iota(jnp.int32, shape, dim)

    def one_if(condition):
        return jnp.where(condition, 1.0, 0.0).astype(F32)

    slot = iota((32, SLOTS), 1)
    x = 2 * (slot >> 5) + ((slot >> 1) & 1)
    y = 2 * ((slot >> 4) & 1) + (slot & 1)
    from_frame = one_if((x * 4 + y) * 2 + ((slot >> 2) & 1) == iota((32, SLOTS), 0))
    frames = dot(jnp.broadcast_to(order.astype(F32), (8, 32)), from_frame)
    tiles = (2.0 * frames + ((iota((8, SLOTS), 1) >> 3) & 1).astype(F32))[0:1]
    is_tile = one_if(iota((SLOTS, SLOTS), 0).astype(F32) == tiles)
    row = iota((8, SLOTS), 0)
    is_own = one_if(iota((8, SLOTS), 1) == block_of(place, core) * TILES + (row & 3))
    own_tiles = dot(is_own, is_tile, NT)
    mask = one_if(mask == 1)
    attends = dot(dot(own_tiles, mask), is_tile)
    attended = dot(dot(own_tiles, mask, NT), is_tile)
    allowed = jnp.where(row < TILES, attends, attended)
    ahead = dot(allowed, one_if(iota((SLOTS, SLOTS), 0) < iota((SLOTS, SLOTS), 1)))
    count = jnp.sum(allowed, axis=1, keepdims=True)
    ahead = jnp.where(allowed > 0.5, ahead, -1.0)
    place_in_list = iota((LANES, SLOTS), 0).astype(F32)
    slots = iota((8, SLOTS), 1).astype(F32)
    lists = jnp.zeros((8, LANES), F32)
    rows, lanes = iota((8, LANES), 0), iota((8, LANES), 1)
    for r in range(8):
        lists = jnp.where(rows == r, dot(slots, one_if(place_in_list == ahead[r : r + 1]), NT), lists)
    lists = jnp.where(lanes.astype(F32) < count, lists, lists[:, 0:1])
    return jnp.where(lanes == LANES - 1, count, lists).astype(jnp.int32)


def enter_kernel(q_ref, k_ref, v_ref, g_ref, mask_ref, order_ref, kv_ref, qg_ref, kv_own, qg_own, list_ref,
                 q_buf, k_buf, v_buf, g_buf, mask_buf, order_buf, kv_pack, qg_pack, load_sems,
                 pair_send, pair_recv, *gather_sems):
    place, core = here()
    wait_all = greet(
        [pair_device(place, core, o) for o in OFFSETS]
        + [mirror_device(place, core, a) for a in range(3)]
        + [device(place, 1 - core)]
    )
    loads = [
        pltpu.make_async_copy(source, target, load_sems.at[i])
        for i, (source, target) in enumerate([
            (k_ref, k_buf), (v_ref, v_buf), (q_ref, q_buf), (g_ref, g_buf),
            (mask_ref, mask_buf), (order_ref, order_buf),
        ])
    ]
    for load in loads:
        load.start()
    own = block_of(place, core)
    packs, whole = (kv_pack, qg_pack), (kv_ref, qg_ref)

    def pair_copy(which, i, arriving=False):
        rows = entry_rows(place, OFFSETS[i] if arriving else (0, 0, 0))
        return remote(packs[which].at[head_of(place, OFFSETS[i])], whole[which].at[own, pl.ds(rows, ROWS), :],
                      pair_send.at[which, i], pair_recv.at[which, i], pair_device(place, core, OFFSETS[i]))

    def hand_out(which):
        for i in range(7):
            pair_copy(which, i).start()
        here_too = packs[which][head_of(place, (0, 0, 0))]
        whole[which][own, pl.ds(entry_rows(place), ROWS), :] = here_too

    gathers = [CubeGather(whole[i], place, core, gather_sems[4 * i : 4 * i + 4]) for i in range(2)]
    loads[0].wait()
    loads[1].wait()
    pack_heads(k_buf, v_buf, kv_pack)
    wait_all()
    hand_out(0)
    loads[2].wait()
    loads[3].wait()
    pack_heads(q_buf, g_buf, qg_pack, HDIM ** -0.5)
    hand_out(1)
    loads[4].wait()
    loads[5].wait()
    list_ref[...] = slot_lists(mask_buf[...], order_buf[...], place, core)
    for which in range(2):
        for i in range(7):
            pair_copy(which, i, True).wait_recv()
        gathers[which].begin()
        (kv_own, qg_own)[which][...] = whole[which][own]
    for k, onward in ((0, (2, 4)), (1, (5,)), (2, (6,)), (3, ()), (4, ()), (5, ()), (6, ())):
        for gather in gathers:
            gather.relay_step(k, onward)
    for which in range(2):
        for i in range(7):
            pair_copy(which, i).wait_send()
    for gather in gathers:
        gather.finish()


def enter(q, k, v, g, tile_mask, frame_order):
    entry = pltpu.VMEM((ROWS, HEADS * HDIM), BF16)
    pack = pltpu.VMEM((HEADS, ROWS, LANES), BF16)
    return pl.pallas_call(
        enter_kernel,
        name="enter",
        out_shape=(
            jax.ShapeDtypeStruct((BLOCKS, BLOCK, LANES), BF16),
            jax.ShapeDtypeStruct((BLOCKS, BLOCK, LANES), BF16),
            jax.ShapeDtypeStruct((BLOCK, LANES), BF16),
            jax.ShapeDtypeStruct((BLOCK, LANES), BF16),
            jax.ShapeDtypeStruct((8, LANES), jnp.int32),
        ),
        in_specs=[HBM_SPEC] * 6,
        out_specs=(VMEM_SPEC,) * 5,
        scratch_shapes=[entry] * 4 + [
            pltpu.VMEM(tile_mask.shape, jnp.int32),
            pltpu.VMEM((1, frame_order.shape[0]), jnp.int32),
            pack,
            pack,
            pltpu.SemaphoreType.DMA((6,)),
            pltpu.SemaphoreType.DMA((2, 7)),
            pltpu.SemaphoreType.DMA((2, 7)),
        ] + GATHER_SEMS * 2,
        compiler_params=pltpu.CompilerParams(
            collective_id=0, has_side_effects=True, vmem_limit_bytes=16 * 2**20
        ),
    )(*[pltpu.with_memory_space_constraint(a, pltpu.HBM) for a in (q, k, v, g, tile_mask, frame_order.reshape(1, -1))])


def share_kernel(stat_own, stat_ref, send, recv):
    place, core = here()
    peers = [(o, c) for o in ALL_OFFSETS for c in (0, 1)][1:]

    def peer_device(offset, flip):
        mirrored = [3 - v if d else v for v, d in zip(place, offset)]
        return device(mirrored, (core + flip) % 2)

    wait_all = greet([peer_device(*p) for p in peers])
    own = block_of(place, core)
    stat_ref[own] = stat_own[...]

    def stat_copy(i, arriving=False):
        offset, flip = peers[i]
        source = block_of(place, (core + flip) % 2, offset) if arriving else own
        part = stat_ref.at[source]
        return remote(part, part, send.at[i], recv.at[i], peer_device(offset, flip))

    wait_all()
    for i in range(15):
        stat_copy(i).start()
    for i in range(15):
        stat_copy(i, True).wait_recv()
    for i in range(15):
        stat_copy(i).wait_send()


def share(stat_own):
    return pl.pallas_call(
        share_kernel,
        name="share",
        out_shape=jax.ShapeDtypeStruct((BLOCKS, 8, LANES), F32),
        in_specs=[VMEM_SPEC],
        out_specs=VMEM_SPEC,
        scratch_shapes=[pltpu.SemaphoreType.DMA((15,)), pltpu.SemaphoreType.DMA((15,))],
        compiler_params=pltpu.CompilerParams(
            collective_id=1, has_side_effects=True, vmem_limit_bytes=4 * 2**20
        ),
    )(stat_own)


def query_kernel(kv_ref, qg_own, list_ref, stat_ref, dq_ref, score_buf, stat_buf):
    low = low_lanes(TILE)
    lane = lax.broadcasted_iota(jnp.int32, (TILE, LANES), 1)
    zero = jnp.zeros((TILE, LANES), BF16)
    zeros = jnp.zeros((TILE, LANES), F32)

    def one_tile(t, unused):
        count = list_ref[t, LANES - 1]
        steps = (count + GROUP - 1) // GROUP
        both = qg_own[t]
        query = jnp.where(low, both, zero)
        grad = jnp.where(low, zero, both)

        def keys_of(step):
            return jnp.concatenate([kv_ref[list_ref[t, step * GROUP + u]] for u in range(GROUP)], axis=0)

        def cut(wide, u):
            return wide[:, u * TILE : (u + 1) * TILE]

        def scores_step(step, peak):
            scores = lax.dot_general(query, keys_of(step), NT, preferred_element_type=F32)
            score_buf[step] = scores
            for u in range(GROUP):
                peak = jnp.maximum(peak, cut(scores, u))
            return peak

        peak = lax.fori_loop(0, steps, scores_step, jnp.full((TILE, LANES), -BIG, F32))
        peak = jnp.max(peak, axis=1, keepdims=True)

        def exp_step(step, mass):
            for u in range(GROUP):
                less = jnp.where(step * GROUP + u < count, 0.0, BIG).astype(F32)
                columns = slice(u * TILE, (u + 1) * TILE)
                term = jnp.exp(score_buf[step, :, columns] - (peak + less))
                score_buf[step, :, columns] = term
                mass = mass + term
            return mass

        mass = lax.fori_loop(0, steps, exp_step, zeros)
        mass = jnp.sum(mass, axis=1, keepdims=True)
        inverse = 1.0 / mass
        log_mass = peak + jnp.log(mass)

        def out_step(step, out):
            probs = (score_buf[step] * inverse).astype(BF16)
            return out + lax.dot_general(probs, keys_of(step), NN, preferred_element_type=F32)

        out = lax.fori_loop(0, steps, out_step, zeros)
        out = out.astype(BF16).astype(F32)
        delta = jnp.sum(jnp.where(low, 0.0, both.astype(F32) * out), axis=1, keepdims=True)

        def grad_step(step, acc):
            keys = keys_of(step)
            prob_grad = lax.dot_general(grad, keys, NT, preferred_element_type=F32)
            score_grad = ((score_buf[step] * inverse) * (prob_grad - delta)).astype(BF16)
            return acc + lax.dot_general(score_grad, keys, NN, preferred_element_type=F32)

        acc = lax.fori_loop(0, steps, grad_step, zeros) * HDIM ** -0.5
        low_part = low_lanes(ROWS // 2)
        for i in range(2):
            top = acc[i * ROWS : i * ROWS + ROWS // 2]
            bottom = acc[i * ROWS + ROWS // 2 : (i + 1) * ROWS]
            dq_ref[2 * t + i] = jnp.where(low_part, top, pltpu.roll(bottom, HDIM, 1)).astype(BF16)
        stats = jnp.where(lane == t, log_mass, stat_buf[...])
        stat_buf[...] = jnp.where(lane == TILES + t, delta, stats)
        return unused

    stat_buf[...] = zeros
    lax.fori_loop(0, TILES, one_tile, 0)
    stat_ref[...] = stat_buf[...].T[:8]


def query_side(kv, qg_own, lists):
    return pl.pallas_call(
        query_kernel,
        name="query_side",
        out_shape=(
            jax.ShapeDtypeStruct((8, LANES), F32),
            jax.ShapeDtypeStruct((2 * TILES, ROWS // 2, LANES), BF16),
        ),
        in_specs=[VMEM_SPEC, VMEM_SPEC, SMEM_SPEC],
        out_specs=(VMEM_SPEC,) * 2,
        scratch_shapes=[
            pltpu.VMEM((SLOTS // GROUP, TILE, GROUP * TILE), F32),
            pltpu.VMEM((TILE, LANES), F32),
        ],
        compiler_params=pltpu.CompilerParams(vmem_limit_bytes=24 * 2**20),
    )(kv.reshape(SLOTS, TILE, LANES), qg_own.reshape(TILES, TILE, LANES), lists)


def key_kernel(qg_ref, stat_ref, kv_own, list_ref, dkv_ref, rows_ref):
    for b in range(BLOCKS):
        for t in range(TILES):
            rows_ref[b * TILES + t, 0:1, :] = stat_ref[b, t : t + 1, :]
            rows_ref[b * TILES + t, 1:2, :] = stat_ref[b, TILES + t : TILES + t + 1, :]
    low = low_lanes(TILE)
    zero = jnp.zeros((TILE, LANES), BF16)

    def one_tile(t, unused):
        count = list_ref[TILES + t, LANES - 1]
        steps = (count + GROUP - 1) // GROUP
        both = kv_own[t]
        stacked = jnp.concatenate([jnp.where(low, both, zero), jnp.where(low, zero, both)], axis=0)

        def step_terms(step, acc):
            lefts, rights = [], []
            for u in range(GROUP):
                slot = list_ref[TILES + t, step * GROUP + u]
                less = jnp.where(step * GROUP + u < count, 0.0, BIG).astype(F32)
                queries = qg_ref[slot]
                products = lax.dot_general(stacked, queries, NT, preferred_element_type=F32)
                probs = jnp.exp(products[:TILE] - (rows_ref[slot, 0:1, :] + less))
                score_grad = probs * (products[TILE:] - rows_ref[slot, 1:2, :])
                lefts += [score_grad.astype(BF16), probs.astype(BF16)]
                rights += [jnp.where(low, queries, zero), jnp.where(low, zero, queries)]
            return acc + lax.dot_general(
                jnp.concatenate(lefts, axis=1), jnp.concatenate(rights, axis=0), NN,
                preferred_element_type=F32,
            )

        acc = lax.fori_loop(0, steps, step_terms, jnp.zeros((TILE, LANES), F32))
        dkv_ref[t] = acc.astype(BF16)
        return unused

    lax.fori_loop(0, TILES, one_tile, 0)


def key_side(qg, stats, kv_own, lists):
    return pl.pallas_call(
        key_kernel,
        name="key_side",
        out_shape=jax.ShapeDtypeStruct((TILES, TILE, LANES), BF16),
        in_specs=[VMEM_SPEC, VMEM_SPEC, VMEM_SPEC, SMEM_SPEC],
        out_specs=VMEM_SPEC,
        scratch_shapes=[
            pltpu.VMEM((SLOTS, 8, LANES), F32),
        ],
        compiler_params=pltpu.CompilerParams(vmem_limit_bytes=24 * 2**20),
    )(qg.reshape(SLOTS, TILE, LANES), stats, kv_own.reshape(TILES, TILE, LANES), lists)


def leave_kernel(dq_ref, dkv_ref, dq_got, dkv_got, pair_send, pair_recv):
    place, core = here()
    wait_all = greet([pair_device(place, core, o) for o in OFFSETS])
    mine = head_of(place, (0, 0, 0))
    sources, landings = (dq_ref, dkv_ref), (dq_got, dkv_got)

    def share_of(offset):
        bits = [(v % 2 + d) % 2 for v, d in zip(place, offset)]
        return (bits[0] * 2 + bits[1]) * 2 + bits[2]

    def pair_copy(which, i, arriving=False):
        landing = landings[which].at[head_of(place, OFFSETS[i]) if arriving else mine]
        return remote(sources[which].at[share_of(OFFSETS[i])], landing,
                      pair_send.at[which, i], pair_recv.at[which, i], pair_device(place, core, OFFSETS[i]))

    wait_all()
    for which in (0, 1):
        for i in range(7):
            pair_copy(which, i).start()
    dq_got[mine] = dq_ref[share_of((0, 0, 0))]
    dkv_got[mine] = dkv_ref[share_of((0, 0, 0))]
    for which in (0, 1):
        for i in range(7):
            pair_copy(which, i, True).wait_recv()
    for which in (0, 1):
        for i in range(7):
            pair_copy(which, i).wait_send()


def unpack_kernel(dq_got, dkv_got, q_ref, k_ref, v_ref, q_out, k_out, v_out, sems):
    def halves(got, j):
        one, two = got[2 * j].astype(F32), got[2 * j + 1].astype(F32)
        low = low_lanes(one.shape[0])
        return (
            jnp.where(low, one, pltpu.roll(two, HDIM, 1)).astype(BF16),
            jnp.where(low, pltpu.roll(one, HDIM, 1), two).astype(BF16),
        )

    for j in range(HEADS // 2):
        columns = slice(j * LANES, (j + 1) * LANES)
        k_out[:, columns], v_out[:, columns] = halves(dkv_got, j)
        q_out[0 : ROWS // 2, columns], q_out[ROWS // 2 : ROWS, columns] = halves(dq_got, j)
    copies = [
        pltpu.make_async_copy(source, target, sems.at[i])
        for i, (source, target) in enumerate([(q_out, q_ref), (k_out, k_ref), (v_out, v_ref)])
    ]
    for copy in copies:
        copy.start()
    for copy in copies:
        copy.wait()


def leave(dq, dkv):
    got = pl.pallas_call(
        leave_kernel,
        name="leave",
        out_shape=(
            jax.ShapeDtypeStruct((HEADS, ROWS // 2, LANES), BF16),
            jax.ShapeDtypeStruct((HEADS, ROWS, LANES), BF16),
        ),
        in_specs=[VMEM_SPEC] * 2,
        out_specs=(VMEM_SPEC,) * 2,
        scratch_shapes=[pltpu.SemaphoreType.DMA((2, 7)), pltpu.SemaphoreType.DMA((2, 7))],
        compiler_params=pltpu.CompilerParams(
            collective_id=2, has_side_effects=True, vmem_limit_bytes=8 * 2**20
        ),
    )(dq, dkv.reshape(HEADS, ROWS, LANES))
    shape = (ROWS, HEADS * HDIM)
    return pl.pallas_call(
        unpack_kernel,
        name="unpack",
        out_shape=(jax.ShapeDtypeStruct(shape, BF16),) * 3,
        in_specs=[VMEM_SPEC] * 2,
        out_specs=(HBM_SPEC,) * 3,
        scratch_shapes=[pltpu.VMEM(shape, BF16)] * 3 + [pltpu.SemaphoreType.DMA((3,))],
        compiler_params=pltpu.CompilerParams(vmem_limit_bytes=8 * 2**20),
    )(*got)


def body(queries, keys, values, out_grad, tile_mask, frame_order):
    kv, qg, kv_own, qg_own, lists = enter(queries, keys, values, out_grad, tile_mask, frame_order)
    stats_own, dq = query_side(kv, qg_own, lists)
    dkv = key_side(qg, share(stats_own), kv_own, lists)
    return leave(dq, dkv)


def solution(mesh):
    whole = P(("blk", "head"), None)
    return jax.shard_map(
        body,
        mesh=mesh,
        in_specs=(whole,) * 4 + (P(), P()),
        out_specs=(whole,) * 3,
        check_vma=False,
    )
```

time: 85.3 us -> 63.8 us (0.75); the launches traced: 83.7 us -> 63.7 us
  Pallas kernels: 76.3 us -> 63 us
  local copies, waits for them, and re-layouts: 6.66 us -> 0 us
    pallas_call x1 -> x2, Pallas kernels: 20.6 us -> 13.5 us  [the longest x1 12.7 us: share(): pl.pallas_call(share_kernel, name='share', out_shape=jax.ShapeDtypeStruct...]
    unnamed x19 -> x0, local copies, waits for them, and re-layouts: 6.66 us -> none
    pallas_call x1, Pallas kernels: 15.6 us -> 9.63 us  [query_side(): pl.pallas_call(query_kernel, name='query_side', out_shape=(jax.ShapeDtype...]
    pallas_call x1, Pallas kernels: 25.1 us -> 28.7 us  [enter(): pl.pallas_call(enter_kernel, name='enter', out_shape=(jax.ShapeDtypeStruc...]
    pallas_call x1, Pallas kernels: 7.2 us -> 4.35 us  [key_side(): pl.pallas_call(key_kernel, name='key_side', out_shape=jax.ShapeDtypeStruc...]
    pallas_call x1, Pallas kernels: 7.83 us -> 6.84 us  [leave(): pl.pallas_call(leave_kernel, name='leave', out_shape=(jax.ShapeDtypeStruc...]
where the time goes in v2:
time: 63.8 us; the launch traced here: 63.7 us
  Pallas kernels  63 us (99%)
  between operations  0.66 us (1%)
    pallas_call x1, Pallas kernels, enter(): pl.pallas_call(enter_kernel, name='enter', out_shape=(jax.ShapeDtypeStruc...  28.7 us
    pallas_call x1, Pallas kernels, share(): pl.pallas_call(share_kernel, name='share', out_shape=jax.ShapeDtypeStruct...  12.7 us
    pallas_call x1, Pallas kernels, query_side(): pl.pallas_call(query_kernel, name='query_side', out_shape=(jax.ShapeDtype...  9.63 us
    pallas_call x1, Pallas kernels, leave(): pl.pallas_call(leave_kernel, name='leave', out_shape=(jax.ShapeDtypeStruc...  6.84 us
    pallas_call x1, Pallas kernels, key_side(): pl.pallas_call(key_kernel, name='key_side', out_shape=jax.ShapeDtypeStruc...  4.35 us

profile of v2, /device:TPU:0, one launch (start us, length us, event | category | flops | bytes accessed | tf_op | source)
XLA Modules:
  0.0 63.7 jit_solution(6051417614133285984)
XLA Ops:
  0.6 28.7 %enter.1 = (bf16[16,512,128]{2,1,0:T(8,128)(2,1)S(1)}, bf16[16,512,128]{2,1,0:T(8,128)(2,1)S(1)}, bf16[512,128]{1,0:T(8,128)(2,1)S(1)}, bf16[512,128]{1,0:T(8,128)(2,1)S(1)}, s32[8,128]{1,0:T(8,128)S(1)}) custom-call(bf16[64,512]{1,0:T(8,128)(2,1)} %q_ref.1, bf16[64,512]{1,0:T(8,128)(2,1)} %k_ref.1, bf16[64,512]{1,0:T(8,128)(2,1)} %v_ref.1, ...), custom_call_target="tpu_custom_call" | custom-call | tf_op jit(solution)/shard_map/enter/pallas_call | solution.py:275
  29.4 9.6 %query_side.1 = (f32[8,128]{1,0:T(8,128)S(1)}, bf16[8,32,128]{2,1,0:T(8,128)(2,1)S(1)}) custom-call(bf16[64,128,128]{2,1,0:T(8,128)(2,1)S(1)} %bitcast.7, bf16[4,128,128]{2,1,0:T(8,128)(2,1)S(1)} %bitcast.10, s32[8,128]{1,0:T(8,128)S(1)} %get-tuple-element.14.list_ref), custom_call_target="tpu_custom_call" | custom-call | tf_op jit(solution)/shard_map/query_side/pallas_call | solution.py:416
  39.0 12.7 %share.1.stat_ref = f32[16,8,128]{2,1,0:T(8,128)S(1)} custom-call(f32[8,128]{1,0:T(8,128)S(1)} %get-tuple-element.17.stat_own), custom_call_target="tpu_custom_call" | custom-call | tf_op jit(solution)/shard_map/share/pallas_call | solution.py:330
  51.7 4.3 %key_side.1 = bf16[4,128,128]{2,1,0:T(8,128)(2,1)S(1)} custom-call(bf16[64,128,128]{2,1,0:T(8,128)(2,1)S(1)} %bitcast.6, f32[16,8,128]{2,1,0:T(8,128)S(1)} %share.1.stat_ref, bf16[4,128,128]{2,1,0:T(8,128)(2,1)S(1)} %bitcast.9, s32[8,128]{1,0:T(8,128)S(1)} %get-tuple-element.14.list_ref), custom_call_target="tpu_custom_call" | custom-call | tf_op jit(solution)/shard_map/key_side/pallas_call | solution.py:471
  56.0 6.8 %leave.1 = (bf16[8,32,128]{2,1,0:T(8,128)(2,1)S(1)}, bf16[8,64,128]{2,1,0:T(8,128)(2,1)S(1)}) custom-call(bf16[8,32,128]{2,1,0:T(8,128)(2,1)S(1)} %get-tuple-element.15.dq_ref, bf16[8,64,128]{2,1,0:T(8,128)(2,1)S(1)} %bitcast.8), custom_call_target="tpu_custom_call" | custom-call | tf_op jit(solution)/shard_map/leave/pallas_call | solution.py:537
  62.9 0.8 %unpack.1 = (bf16[64,512]{1,0:T(8,128)(2,1)}, bf16[64,512]{1,0:T(8,128)(2,1)}, bf16[64,512]{1,0:T(8,128)(2,1)}) custom-call(bf16[8,32,128]{2,1,0:T(8,128)(2,1)S(1)} %get-tuple-element.19.dq_got, bf16[8,64,128]{2,1,0:T(8,128)(2,1)S(1)} %get-tuple-element.20.dkv_got), custom_call_target="tpu_custom_call" | custom-call | tf_op jit(solution)/shard_map/unpack/pallas_call | solution.py:552

commit v3 on v2

--- a/solution.py
+++ b/solution.py
@@ -16,7 +16,10 @@
 BLOCK = TILES * TILE
 BLOCKS = 16
 SLOTS = BLOCKS * TILES
-GROUP = 8
+GROUP = 24
+KEY_GROUP = 24
+SPAN = 4
+KEY_SPAN = 4
 PIECES = ((0, 176), (176, 176), (352, 160))
 MESH = pl.DeviceIdType.MESH
 F32 = jnp.float32
@@ -29,50 +32,57 @@
 SMEM_SPEC = pl.BlockSpec(memory_space=pltpu.SMEM)
 
 
-def here():
-    blk = lax.axis_index("blk")
-    z = lax.axis_index("head")
-    return (blk // 8, (blk // 2) % 4, z), blk % 2
-
-
-def device(place, core):
-    x, y, z = place
-    return ((x * 4 + y) * 2 + core, z)
-
-
-def paired(v, flip):
-    return v + (1 - 2 * (v % 2)) if flip else v
-
-
-def half(v):
-    return ((v + 1) // 2) % 2
-
-
-def head_of(place, offset):
-    bits = [(half(v) + d) % 2 for v, d in zip(place, offset)]
-    return bits[0] * 4 + bits[1] * 2 + bits[2]
-
-
-def block_of(place, core, offset=(0, 0, 0)):
-    bits = [(v // 2 + d) % 2 for v, d in zip(place, offset)]
-    return ((bits[0] * 2 + bits[1]) * 2 + bits[2]) * 2 + core
-
-
-def entry_rows(place, offset=(0, 0, 0)):
-    bits = [(v % 2 + d) % 2 for v, d in zip(place, offset)]
-    return pl.multiple_of((bits[0] * 2 + bits[1]) * TILE + bits[2] * ROWS, ROWS)
+class Place:
+    def __init__(self):
+        blk = lax.axis_index("blk")
+        z = lax.axis_index("head")
+        x = blk // 8
+        rest = blk - 8 * x
+        y = rest // 2
+        self.core = rest - 2 * y
+        self.other = 1 - self.core
+        self.at = (x, y, z)
+        self.high = [(h, 1 - h) for h in (v // 2 for v in self.at)]
+        self.low = [(l, 1 - l) for l in (v - 2 * h[0] for v, h in zip(self.at, self.high))]
+        halves = [h[0] + l[0] - 2 * h[0] * l[0] for h, l in zip(self.high, self.low)]
+        self.half = [(h, 1 - h) for h in halves]
+        self.pair = [(v, v + 1 - 2 * l[0]) for v, l in zip(self.at, self.low)]
+        self.mirror = [(v, 3 - v) for v in self.at]
+        self.known = {}
+
+    def once(self, key, work):
+        if key not in self.known:
+            self.known[key] = work()
+        return self.known[key]
+
+    def device(self, table, offset, flip):
+        x, y, z = [t[d] for t, d in zip(table, offset)]
+        return ((x * 4 + y) * 2 + (self.other if flip else self.core), z)
+
+    def pair_device(self, offset):
+        return self.once(("pair", offset), lambda: self.device(self.pair, offset, 0))
+
+    def mirror_device(self, offset, flip=0):
+        return self.once(("mirror", offset, flip), lambda: self.device(self.mirror, offset, flip))
+
+    def number(self, bits, offset):
+        return (bits[0][offset[0]] * 2 + bits[1][offset[1]]) * 2 + bits[2][offset[2]]
+
+    def head(self, offset=(0, 0, 0)):
+        return self.once(("head", offset), lambda: self.number(self.half, offset))
+
+    def entry(self, offset=(0, 0, 0)):
+        return self.once(("entry", offset), lambda: self.number(self.low, offset))
+
+    def block(self, offset=(0, 0, 0), flip=0):
+        return self.once(
+            ("block", offset, flip),
+            lambda: self.number(self.high, offset) * 2 + (self.other if flip else self.core),
+        )
 
 
 ALL_OFFSETS = [(a, b, c) for a in (0, 1) for b in (0, 1) for c in (0, 1)]
 OFFSETS = ALL_OFFSETS[1:]
-
-
-def pair_device(place, core, offset):
-    return device([paired(v, d) for v, d in zip(place, offset)], core)
-
-
-def mirror_device(place, core, axis):
-    return device([3 - v if a == axis else v for a, v in enumerate(place)], core)
 
 
 def remote(src, dst, send, recv, target):
@@ -96,8 +106,8 @@
 
 
 class CubeGather:
-    def __init__(self, ref, place, core, sems):
-        self.ref, self.place, self.core = ref, place, core
+    def __init__(self, ref, place, sems):
+        self.ref, self.place = ref, place
         self.send, self.recv, self.core_send, self.core_recv = sems
         self.pieces = [0] * len(ALL_OFFSETS)
 
@@ -111,15 +121,14 @@
         if arriving:
             offset = plus(offset, UNIT[axis])
         first, count = PIECES[piece]
-        part = self.ref.at[block_of(self.place, self.core, offset), pl.ds(first, count), :]
+        part = self.ref.at[self.place.block(offset), pl.ds(first, count), :]
         return remote(part, part, self.send.at[piece, k], self.recv.at[piece, k],
-                      mirror_device(self.place, self.core, axis))
+                      self.place.mirror_device(UNIT[axis]))
 
     def core_copy(self, i, arriving=False):
-        core = 1 - self.core if arriving else self.core
-        part = self.ref.at[block_of(self.place, core, ALL_OFFSETS[i])]
+        part = self.ref.at[self.place.block(ALL_OFFSETS[i], int(arriving))]
         return remote(part, part, self.core_send.at[i], self.core_recv.at[i],
-                      device(self.place, 1 - self.core))
+                      self.place.mirror_device((0, 0, 0), 1))
 
     def begin(self):
         for k in (0, 1, 3):
@@ -148,6 +157,11 @@
             self.core_copy(i).wait_send()
 
 
+def entry_rows(place, offset=(0, 0, 0)):
+    bits = [place.low[a][d] for a, d in enumerate(offset)]
+    return pl.ds(pl.multiple_of((bits[0] * 2 + bits[1]) * TILE + bits[2] * ROWS, ROWS), ROWS)
+
+
 GATHER_SEMS = [
     pltpu.SemaphoreType.DMA((3, 7)),
     pltpu.SemaphoreType.DMA((3, 7)),
@@ -172,7 +186,7 @@
         packed[2 * j + 1] = jnp.where(low, pltpu.roll(one, HDIM, 1), two).astype(BF16)
 
 
-def slot_lists(mask, order, place, core):
+def slot_lists(mask, order, place):
     def dot(a, b, dims=NN):
         return lax.dot_general(a.astype(BF16), b.astype(BF16), dims, preferred_element_type=F32)
 
@@ -190,7 +204,7 @@
     tiles = (2.0 * frames + ((iota((8, SLOTS), 1) >> 3) & 1).astype(F32))[0:1]
     is_tile = one_if(iota((SLOTS, SLOTS), 0).astype(F32) == tiles)
     row = iota((8, SLOTS), 0)
-    is_own = one_if(iota((8, SLOTS), 1) == block_of(place, core) * TILES + (row & 3))
+    is_own = one_if(iota((8, SLOTS), 1) == place.block() * TILES + (row & 3))
     own_tiles = dot(is_own, is_tile, NT)
     mask = one_if(mask == 1)
     attends = dot(dot(own_tiles, mask), is_tile)
@@ -212,11 +226,11 @@
 def enter_kernel(q_ref, k_ref, v_ref, g_ref, mask_ref, order_ref, kv_ref, qg_ref, kv_own, qg_own, list_ref,
                  q_buf, k_buf, v_buf, g_buf, mask_buf, order_buf, kv_pack, qg_pack, load_sems,
                  pair_send, pair_recv, *gather_sems):
-    place, core = here()
+    place = Place()
     wait_all = greet(
-        [pair_device(place, core, o) for o in OFFSETS]
-        + [mirror_device(place, core, a) for a in range(3)]
-        + [device(place, 1 - core)]
+        [place.pair_device(o) for o in OFFSETS]
+        + [place.mirror_device(u) for u in UNIT]
+        + [place.mirror_device((0, 0, 0), 1)]
     )
     loads = [
         pltpu.make_async_copy(source, target, load_sems.at[i])
@@ -227,21 +241,21 @@
     ]
     for load in loads:
         load.start()
-    own = block_of(place, core)
+    own = place.block()
     packs, whole = (kv_pack, qg_pack), (kv_ref, qg_ref)
 
     def pair_copy(which, i, arriving=False):
         rows = entry_rows(place, OFFSETS[i] if arriving else (0, 0, 0))
-        return remote(packs[which].at[head_of(place, OFFSETS[i])], whole[which].at[own, pl.ds(rows, ROWS), :],
-                      pair_send.at[which, i], pair_recv.at[which, i], pair_device(place, core, OFFSETS[i]))
+        return remote(packs[which].at[place.head(OFFSETS[i])], whole[which].at[own, rows, :],
+                      pair_send.at[which, i], pair_recv.at[which, i], place.pair_device(OFFSETS[i]))
 
     def hand_out(which):
         for i in range(7):
             pair_copy(which, i).start()
-        here_too = packs[which][head_of(place, (0, 0, 0))]
-        whole[which][own, pl.ds(entry_rows(place), ROWS), :] = here_too
-
-    gathers = [CubeGather(whole[i], place, core, gather_sems[4 * i : 4 * i + 4]) for i in range(2)]
+        here_too = packs[which][place.head()]
+        whole[which][own, entry_rows(place), :] = here_too
+
+    gathers = [CubeGather(whole[i], place, gather_sems[4 * i : 4 * i + 4]) for i in range(2)]
     loads[0].wait()
     loads[1].wait()
     pack_heads(k_buf, v_buf, kv_pack)
@@ -253,7 +267,7 @@
     hand_out(1)
     loads[4].wait()
     loads[5].wait()
-    list_ref[...] = slot_lists(mask_buf[...], order_buf[...], place, core)
+    list_ref[...] = slot_lists(mask_buf[...], order_buf[...], place)
     for which in range(2):
         for i in range(7):
             pair_copy(which, i, True).wait_recv()
@@ -300,22 +314,18 @@
 
 
 def share_kernel(stat_own, stat_ref, send, recv):
-    place, core = here()
+    place = Place()
     peers = [(o, c) for o in ALL_OFFSETS for c in (0, 1)][1:]
 
-    def peer_device(offset, flip):
-        mirrored = [3 - v if d else v for v, d in zip(place, offset)]
-        return device(mirrored, (core + flip) % 2)
-
-    wait_all = greet([peer_device(*p) for p in peers])
-    own = block_of(place, core)
+    wait_all = greet([place.mirror_device(*p) for p in peers])
+    own = place.block()
     stat_ref[own] = stat_own[...]
 
     def stat_copy(i, arriving=False):
         offset, flip = peers[i]
-        source = block_of(place, (core + flip) % 2, offset) if arriving else own
+        source = place.block(offset, flip) if arriving else own
         part = stat_ref.at[source]
-        return remote(part, part, send.at[i], recv.at[i], peer_device(offset, flip))
+        return remote(part, part, send.at[i], recv.at[i], place.mirror_device(offset, flip))
 
     wait_all()
     for i in range(15):
@@ -340,75 +350,104 @@
     )(stat_own)
 
 
-def query_kernel(kv_ref, qg_own, list_ref, stat_ref, dq_ref, score_buf, stat_buf):
+def query_kernel(kv_ref, qg_own, list_ref, stat_ref, dq_ref, term_buf, peak_buf, stat_buf):
     low = low_lanes(TILE)
     lane = lax.broadcasted_iota(jnp.int32, (TILE, LANES), 1)
     zero = jnp.zeros((TILE, LANES), BF16)
     zeros = jnp.zeros((TILE, LANES), F32)
 
-    def one_tile(t, unused):
-        count = list_ref[t, LANES - 1]
-        steps = (count + GROUP - 1) // GROUP
-        both = qg_own[t]
-        query = jnp.where(low, both, zero)
-        grad = jnp.where(low, zero, both)
-
-        def keys_of(step):
-            return jnp.concatenate([kv_ref[list_ref[t, step * GROUP + u]] for u in range(GROUP)], axis=0)
-
-        def cut(wide, u):
-            return wide[:, u * TILE : (u + 1) * TILE]
-
-        def scores_step(step, peak):
-            scores = lax.dot_general(query, keys_of(step), NT, preferred_element_type=F32)
-            score_buf[step] = scores
-            for u in range(GROUP):
-                peak = jnp.maximum(peak, cut(scores, u))
-            return peak
-
-        peak = lax.fori_loop(0, steps, scores_step, jnp.full((TILE, LANES), -BIG, F32))
-        peak = jnp.max(peak, axis=1, keepdims=True)
-
-        def exp_step(step, mass):
-            for u in range(GROUP):
-                less = jnp.where(step * GROUP + u < count, 0.0, BIG).astype(F32)
-                columns = slice(u * TILE, (u + 1) * TILE)
-                term = jnp.exp(score_buf[step, :, columns] - (peak + less))
-                score_buf[step, :, columns] = term
-                mass = mass + term
-            return mass
-
-        mass = lax.fori_loop(0, steps, exp_step, zeros)
-        mass = jnp.sum(mass, axis=1, keepdims=True)
-        inverse = 1.0 / mass
-        log_mass = peak + jnp.log(mass)
-
-        def out_step(step, out):
-            probs = (score_buf[step] * inverse).astype(BF16)
-            return out + lax.dot_general(probs, keys_of(step), NN, preferred_element_type=F32)
-
-        out = lax.fori_loop(0, steps, out_step, zeros)
-        out = out.astype(BF16).astype(F32)
-        delta = jnp.sum(jnp.where(low, 0.0, both.astype(F32) * out), axis=1, keepdims=True)
-
-        def grad_step(step, acc):
-            keys = keys_of(step)
-            prob_grad = lax.dot_general(grad, keys, NT, preferred_element_type=F32)
-            score_grad = ((score_buf[step] * inverse) * (prob_grad - delta)).astype(BF16)
-            return acc + lax.dot_general(score_grad, keys, NN, preferred_element_type=F32)
-
-        acc = lax.fori_loop(0, steps, grad_step, zeros) * HDIM ** -0.5
+    def some_tiles(first, unused):
+        span = range(SPAN)
+        tiles = [first * SPAN + i for i in span]
+        counts = [list_ref[t, LANES - 1] for t in tiles]
+        most = functools.reduce(jnp.maximum, counts)
+        steps = (most + GROUP - 1) // GROUP
+        both = [qg_own[t] for t in tiles]
+
+        def keys_of(i, step):
+            return jnp.concatenate([kv_ref[list_ref[tiles[i], step * GROUP + u]] for u in range(GROUP)], axis=0)
+
+        def cut(u):
+            return slice(u * TILE, (u + 1) * TILE)
+
+        def term_step(step, state):
+            after = []
+            for i in span:
+                before, mass = state[2 * i : 2 * i + 2]
+                query = jnp.where(low, both[i], zero)
+                scores = lax.dot_general(query, keys_of(i, step), NT, preferred_element_type=F32)
+                peak = before
+                for u in range(GROUP):
+                    peak = jnp.maximum(peak, scores[:, cut(u)])
+                mass = mass * jnp.exp(before - peak)
+                for u in range(GROUP):
+                    less = jnp.where(step * GROUP + u < counts[i], 0.0, BIG).astype(F32)
+                    term = jnp.exp(scores[:, cut(u)] - (peak + less))
+                    term_buf[i, step, :, cut(u)] = term
+                    mass = mass + term
+                peak_buf[i, step] = peak
+                after += [peak, mass]
+            return tuple(after)
+
+        state = lax.fori_loop(0, steps, term_step, (jnp.full((TILE, LANES), -BIG, F32), zeros) * SPAN)
+        peaks, inverses, log_masses = [], [], []
+        for i in span:
+            lane_peak, lane_mass = state[2 * i : 2 * i + 2]
+            peak = jnp.max(lane_peak, axis=1, keepdims=True)
+            mass = jnp.sum(lane_mass * jnp.exp(lane_peak - peak), axis=1, keepdims=True)
+            peaks.append(peak)
+            inverses.append(1.0 / mass)
+            log_masses.append(peak + jnp.log(mass))
+
+        def out_step(step, outs):
+            after = []
+            for i in span:
+                factor = jnp.exp(peak_buf[i, step] - peaks[i]) * inverses[i]
+                peak_buf[i, step] = factor
+                probs = [(term_buf[i, step, :, cut(u)] * factor).astype(BF16) for u in range(GROUP)]
+                after.append(outs[i] + lax.dot_general(
+                    jnp.concatenate(probs, axis=1), keys_of(i, step), NN, preferred_element_type=F32
+                ))
+            return tuple(after)
+
+        outs = lax.fori_loop(0, steps, out_step, (zeros,) * SPAN)
+        deltas = []
+        for i in span:
+            out = outs[i].astype(BF16).astype(F32)
+            deltas.append(jnp.sum(jnp.where(low, 0.0, both[i].astype(F32) * out), axis=1, keepdims=True))
+
+        def grad_step(step, accs):
+            after = []
+            for i in span:
+                keys = keys_of(i, step)
+                factor = peak_buf[i, step]
+                grad = jnp.where(low, zero, both[i])
+                prob_grad = lax.dot_general(grad, keys, NT, preferred_element_type=F32)
+                score_grad = [
+                    ((term_buf[i, step, :, cut(u)] * factor) * (prob_grad[:, cut(u)] - deltas[i])).astype(BF16)
+                    for u in range(GROUP)
+                ]
+                after.append(accs[i] + lax.dot_general(
+                    jnp.concatenate(score_grad, axis=1), keys, NN, preferred_element_type=F32
+                ))
+            return tuple(after)
+
+        accs = lax.fori_loop(0, steps, grad_step, (zeros,) * SPAN)
         low_part = low_lanes(ROWS // 2)
-        for i in range(2):
-            top = acc[i * ROWS : i * ROWS + ROWS // 2]
-            bottom = acc[i * ROWS + ROWS // 2 : (i + 1) * ROWS]
-            dq_ref[2 * t + i] = jnp.where(low_part, top, pltpu.roll(bottom, HDIM, 1)).astype(BF16)
-        stats = jnp.where(lane == t, log_mass, stat_buf[...])
-        stat_buf[...] = jnp.where(lane == TILES + t, delta, stats)
+        stats = stat_buf[...]
+        for i in span:
+            acc = accs[i] * HDIM ** -0.5
+            for j in range(2):
+                top = acc[j * ROWS : j * ROWS + ROWS // 2]
+                bottom = acc[j * ROWS + ROWS // 2 : (j + 1) * ROWS]
+                dq_ref[2 * tiles[i] + j] = jnp.where(low_part, top, pltpu.roll(bottom, HDIM, 1)).astype(BF16)
+            stats = jnp.where(lane == tiles[i], log_masses[i], stats)
+            stats = jnp.where(lane == TILES + tiles[i], deltas[i], stats)
+        stat_buf[...] = stats
         return unused
 
     stat_buf[...] = zeros
-    lax.fori_loop(0, TILES, one_tile, 0)
+    lax.fori_loop(0, TILES // SPAN, some_tiles, 0)
     stat_ref[...] = stat_buf[...].T[:8]
 
 
@@ -423,7 +462,8 @@
         in_specs=[VMEM_SPEC, VMEM_SPEC, SMEM_SPEC],
         out_specs=(VMEM_SPEC,) * 2,
         scratch_shapes=[
-            pltpu.VMEM((SLOTS // GROUP, TILE, GROUP * TILE), F32),
+            pltpu.VMEM((SPAN, -(-SLOTS // GROUP), TILE, GROUP * TILE), F32),
+            pltpu.VMEM((SPAN, -(-SLOTS // GROUP), TILE, LANES), F32),
             pltpu.VMEM((TILE, LANES), F32),
         ],
         compiler_params=pltpu.CompilerParams(vmem_limit_bytes=24 * 2**20),
@@ -438,33 +478,42 @@
     low = low_lanes(TILE)
     zero = jnp.zeros((TILE, LANES), BF16)
 
-    def one_tile(t, unused):
-        count = list_ref[TILES + t, LANES - 1]
-        steps = (count + GROUP - 1) // GROUP
-        both = kv_own[t]
-        stacked = jnp.concatenate([jnp.where(low, both, zero), jnp.where(low, zero, both)], axis=0)
-
-        def step_terms(step, acc):
-            lefts, rights = [], []
-            for u in range(GROUP):
-                slot = list_ref[TILES + t, step * GROUP + u]
-                less = jnp.where(step * GROUP + u < count, 0.0, BIG).astype(F32)
-                queries = qg_ref[slot]
-                products = lax.dot_general(stacked, queries, NT, preferred_element_type=F32)
-                probs = jnp.exp(products[:TILE] - (rows_ref[slot, 0:1, :] + less))
-                score_grad = probs * (products[TILE:] - rows_ref[slot, 1:2, :])
-                lefts += [score_grad.astype(BF16), probs.astype(BF16)]
-                rights += [jnp.where(low, queries, zero), jnp.where(low, zero, queries)]
-            return acc + lax.dot_general(
-                jnp.concatenate(lefts, axis=1), jnp.concatenate(rights, axis=0), NN,
-                preferred_element_type=F32,
-            )
-
-        acc = lax.fori_loop(0, steps, step_terms, jnp.zeros((TILE, LANES), F32))
-        dkv_ref[t] = acc.astype(BF16)
+    def some_tiles(first, unused):
+        span = range(KEY_SPAN)
+        tiles = [first * KEY_SPAN + i for i in span]
+        counts = [list_ref[TILES + t, LANES - 1] for t in tiles]
+        most = functools.reduce(jnp.maximum, counts)
+        steps = (most + KEY_GROUP - 1) // KEY_GROUP
+        stacks = [
+            jnp.concatenate([jnp.where(low, kv_own[t], zero), jnp.where(low, zero, kv_own[t])], axis=0)
+            for t in tiles
+        ]
+
+        def step_terms(step, accs):
+            after = []
+            for i in span:
+                lefts, rights = [], []
+                for u in range(KEY_GROUP):
+                    slot = list_ref[TILES + tiles[i], step * KEY_GROUP + u]
+                    less = jnp.where(step * KEY_GROUP + u < counts[i], 0.0, BIG).astype(F32)
+                    queries = qg_ref[slot]
+                    products = lax.dot_general(stacks[i], queries, NT, preferred_element_type=F32)
+                    probs = jnp.exp(products[:TILE] - (rows_ref[slot, 0:1, :] + less))
+                    score_grad = probs * (products[TILE:] - rows_ref[slot, 1:2, :])
+                    lefts += [score_grad.astype(BF16), probs.astype(BF16)]
+                    rights += [jnp.where(low, queries, zero), jnp.where(low, zero, queries)]
+                after.append(accs[i] + lax.dot_general(
+                    jnp.concatenate(lefts, axis=1), jnp.concatenate(rights, axis=0), NN,
+                    preferred_element_type=F32,
+                ))
+            return tuple(after)
+
+        accs = lax.fori_loop(0, steps, step_terms, (jnp.zeros((TILE, LANES), F32),) * KEY_SPAN)
+        for i in span:
+            dkv_ref[tiles[i]] = accs[i].astype(BF16)
         return unused
 
-    lax.fori_loop(0, TILES, one_tile, 0)
+    lax.fori_loop(0, TILES // KEY_SPAN, some_tiles, 0)
 
 
 def key_side(qg, stats, kv_own, lists):
@@ -482,26 +531,22 @@
 
 
 def leave_kernel(dq_ref, dkv_ref, dq_got, dkv_got, pair_send, pair_recv):
-    place, core = here()
-    wait_all = greet([pair_device(place, core, o) for o in OFFSETS])
-    mine = head_of(place, (0, 0, 0))
+    place = Place()
+    wait_all = greet([place.pair_device(o) for o in OFFSETS])
+    mine = place.head()
     sources, landings = (dq_ref, dkv_ref), (dq_got, dkv_got)
 
-    def share_of(offset):
-        bits = [(v % 2 + d) % 2 for v, d in zip(place, offset)]
-        return (bits[0] * 2 + bits[1]) * 2 + bits[2]
-
     def pair_copy(which, i, arriving=False):
-        landing = landings[which].at[head_of(place, OFFSETS[i]) if arriving else mine]
-        return remote(sources[which].at[share_of(OFFSETS[i])], landing,
-                      pair_send.at[which, i], pair_recv.at[which, i], pair_device(place, core, OFFSETS[i]))
+        landing = landings[which].at[place.head(OFFSETS[i]) if arriving else mine]
+        return remote(sources[which].at[place.entry(OFFSETS[i])], landing,
+                      pair_send.at[which, i], pair_recv.at[which, i], place.pair_device(OFFSETS[i]))
 
     wait_all()
     for which in (0, 1):
         for i in range(7):
             pair_copy(which, i).start()
-    dq_got[mine] = dq_ref[share_of((0, 0, 0))]
-    dkv_got[mine] = dkv_ref[share_of((0, 0, 0))]
+    dq_got[mine] = dq_ref[place.entry()]
+    dkv_got[mine] = dkv_ref[place.entry()]
     for which in (0, 1):
         for i in range(7):
             pair_copy(which, i, True).wait_recv()

time: 63.8 us -> 57.9 us (0.908)
  Pallas kernels: 63 us -> 57 us
    pallas_call x1, Pallas kernels: 9.63 us -> 6.21 us  [query_side(): pl.pallas_call(query_kernel, name='query_side', out_shape=(jax.ShapeDtype...]
    pallas_call x1, Pallas kernels: 12.7 us -> 9.87 us  [share(): pl.pallas_call(share_kernel, name='share', out_shape=jax.ShapeDtypeStruct...]
where the time goes in v3:
time: 57.9 us; the launch traced here: 57.7 us
  Pallas kernels  57 us (98%)
  between operations  0.66 us (1%)
    pallas_call x1, Pallas kernels, enter(): pl.pallas_call(enter_kernel, name='enter', out_shape=(jax.ShapeDtypeStruc...  28.7 us
    pallas_call x1, Pallas kernels, share(): pl.pallas_call(share_kernel, name='share', out_shape=jax.ShapeDtypeStruct...  9.87 us
    pallas_call x1, Pallas kernels, leave(): pl.pallas_call(leave_kernel, name='leave', out_shape=(jax.ShapeDtypeStruc...  7.05 us
    pallas_call x1, Pallas kernels, query_side(): pl.pallas_call(query_kernel, name='query_side', out_shape=(jax.ShapeDtype...  6.21 us
    pallas_call x1, Pallas kernels, key_side(): pl.pallas_call(key_kernel, name='key_side', out_shape=jax.ShapeDtypeStruc...  4.34 us

profile of v3, /device:TPU:0, one launch (start us, length us, event | category | flops | bytes accessed | tf_op | source)
XLA Modules:
  0.0 57.7 jit_solution(8847012691301645289)
XLA Ops:
  0.6 28.7 %enter.1 = (bf16[16,512,128]{2,1,0:T(8,128)(2,1)S(1)}, bf16[16,512,128]{2,1,0:T(8,128)(2,1)S(1)}, bf16[512,128]{1,0:T(8,128)(2,1)S(1)}, bf16[512,128]{1,0:T(8,128)(2,1)S(1)}, s32[8,128]{1,0:T(8,128)S(1)}) custom-call(bf16[64,512]{1,0:T(8,128)(2,1)} %q_ref.1, bf16[64,512]{1,0:T(8,128)(2,1)} %k_ref.1, bf16[64,512]{1,0:T(8,128)(2,1)} %v_ref.1, ...), custom_call_target="tpu_custom_call" | custom-call | tf_op jit(solution)/shard_map/enter/pallas_call | solution.py:289
  29.4 6.2 %query_side.1 = (f32[8,128]{1,0:T(8,128)S(1)}, bf16[8,32,128]{2,1,0:T(8,128)(2,1)S(1)}) custom-call(bf16[64,128,128]{2,1,0:T(8,128)(2,1)S(1)} %bitcast.7, bf16[4,128,128]{2,1,0:T(8,128)(2,1)S(1)} %bitcast.10, s32[8,128]{1,0:T(8,128)S(1)} %get-tuple-element.14.list_ref), custom_call_target="tpu_custom_call" | custom-call | tf_op jit(solution)/shard_map/query_side/pallas_call | solution.py:455
  35.6 9.9 %share.1.stat_ref = f32[16,8,128]{2,1,0:T(8,128)S(1)} custom-call(f32[8,128]{1,0:T(8,128)S(1)} %get-tuple-element.17.stat_own), custom_call_target="tpu_custom_call" | custom-call | tf_op jit(solution)/shard_map/share/pallas_call | solution.py:340
  45.5 4.3 %key_side.1 = bf16[4,128,128]{2,1,0:T(8,128)(2,1)S(1)} custom-call(bf16[64,128,128]{2,1,0:T(8,128)(2,1)S(1)} %bitcast.6, f32[16,8,128]{2,1,0:T(8,128)S(1)} %share.1.stat_ref, bf16[4,128,128]{2,1,0:T(8,128)(2,1)S(1)} %bitcast.9, s32[8,128]{1,0:T(8,128)S(1)} %get-tuple-element.14.list_ref), custom_call_target="tpu_custom_call" | custom-call | tf_op jit(solution)/shard_map/key_side/pallas_call | solution.py:520
  49.8 7.0 %leave.1 = (bf16[8,32,128]{2,1,0:T(8,128)(2,1)S(1)}, bf16[8,64,128]{2,1,0:T(8,128)(2,1)S(1)}) custom-call(bf16[8,32,128]{2,1,0:T(8,128)(2,1)S(1)} %get-tuple-element.15.dq_ref, bf16[8,64,128]{2,1,0:T(8,128)(2,1)S(1)} %bitcast.8), custom_call_target="tpu_custom_call" | custom-call | tf_op jit(solution)/shard_map/leave/pallas_call | solution.py:582
  56.9 0.8 %unpack.1 = (bf16[64,512]{1,0:T(8,128)(2,1)}, bf16[64,512]{1,0:T(8,128)(2,1)}, bf16[64,512]{1,0:T(8,128)(2,1)}) custom-call(bf16[8,32,128]{2,1,0:T(8,128)(2,1)S(1)} %get-tuple-element.19.dq_got, bf16[8,64,128]{2,1,0:T(8,128)(2,1)S(1)} %get-tuple-element.20.dkv_got), custom_call_target="tpu_custom_call" | custom-call | tf_op jit(solution)/shard_map/unpack/pallas_call | solution.py:597

commit v4 on v3

--- a/solution.py
+++ b/solution.py
@@ -82,7 +82,7 @@
 
 
 ALL_OFFSETS = [(a, b, c) for a in (0, 1) for b in (0, 1) for c in (0, 1)]
-OFFSETS = ALL_OFFSETS[1:]
+OFFSETS = sorted(ALL_OFFSETS[1:], key=sum, reverse=True)
 
 
 def remote(src, dst, send, recv, target):
@@ -108,7 +108,10 @@
 class CubeGather:
     def __init__(self, ref, place, sems):
         self.ref, self.place = ref, place
-        self.send, self.recv, self.core_send, self.core_recv = sems
+        self.forward = len(sems) == 4
+        self.send, self.recv = sems[:2]
+        if self.forward:
+            self.core_send, self.core_recv = sems[2:]
         self.pieces = [0] * len(ALL_OFFSETS)
 
     def hops(self, piece):
@@ -134,7 +137,8 @@
         for k in (0, 1, 3):
             for p in range(3):
                 self.hop_copy(p, k).start()
-        self.core_copy(0).start()
+        if self.forward:
+            self.core_copy(0).start()
 
     def relay_step(self, k, onward):
         for p in range(3):
@@ -144,17 +148,19 @@
             axis, offset = self.hops(p)[k]
             i = ALL_OFFSETS.index(plus(offset, UNIT[axis]))
             self.pieces[i] += 1
-            if self.pieces[i] == 3:
+            if self.forward and self.pieces[i] == 3:
                 self.core_copy(i).start()
 
     def finish(self):
-        for i in range(8):
-            self.core_copy(i, True).wait_recv()
+        if self.forward:
+            for i in range(8):
+                self.core_copy(i, True).wait_recv()
         for p in range(3):
             for k in range(7):
                 self.hop_copy(p, k).wait_send()
-        for i in range(8):
-            self.core_copy(i).wait_send()
+        if self.forward:
+            for i in range(8):
+                self.core_copy(i).wait_send()
 
 
 def entry_rows(place, offset=(0, 0, 0)):
@@ -242,20 +248,24 @@
     for load in loads:
         load.start()
     own = place.block()
-    packs, whole = (kv_pack, qg_pack), (kv_ref, qg_ref)
+    packs, landings = (kv_pack, qg_pack), (kv_ref.at[own], qg_ref.at[own])
 
     def pair_copy(which, i, arriving=False):
         rows = entry_rows(place, OFFSETS[i] if arriving else (0, 0, 0))
-        return remote(packs[which].at[place.head(OFFSETS[i])], whole[which].at[own, rows, :],
+        return remote(packs[which].at[place.head(OFFSETS[i])], landings[which].at[rows, :],
                       pair_send.at[which, i], pair_recv.at[which, i], place.pair_device(OFFSETS[i]))
 
     def hand_out(which):
         for i in range(7):
             pair_copy(which, i).start()
         here_too = packs[which][place.head()]
-        whole[which][own, entry_rows(place), :] = here_too
-
-    gathers = [CubeGather(whole[i], place, gather_sems[4 * i : 4 * i + 4]) for i in range(2)]
+        landings[which][entry_rows(place), :] = here_too
+
+    def taken_in(which):
+        for i in range(7):
+            pair_copy(which, i, True).wait_recv()
+
+    gathers = [CubeGather(kv_ref, place, gather_sems[:4]), CubeGather(qg_ref, place, gather_sems[4:])]
     loads[0].wait()
     loads[1].wait()
     pack_heads(k_buf, v_buf, kv_pack)
@@ -269,10 +279,9 @@
     loads[5].wait()
     list_ref[...] = slot_lists(mask_buf[...], order_buf[...], place)
     for which in range(2):
-        for i in range(7):
-            pair_copy(which, i, True).wait_recv()
+        taken_in(which)
         gathers[which].begin()
-        (kv_own, qg_own)[which][...] = whole[which][own]
+        (kv_own, qg_own)[which][...] = landings[which][...]
     for k, onward in ((0, (2, 4)), (1, (5,)), (2, (6,)), (3, ()), (4, ()), (5, ()), (6, ())):
         for gather in gathers:
             gather.relay_step(k, onward)
@@ -306,48 +315,86 @@
             pltpu.SemaphoreType.DMA((6,)),
             pltpu.SemaphoreType.DMA((2, 7)),
             pltpu.SemaphoreType.DMA((2, 7)),
-        ] + GATHER_SEMS * 2,
+        ] + GATHER_SEMS + GATHER_SEMS[:2],
         compiler_params=pltpu.CompilerParams(
             collective_id=0, has_side_effects=True, vmem_limit_bytes=16 * 2**20
         ),
     )(*[pltpu.with_memory_space_constraint(a, pltpu.HBM) for a in (q, k, v, g, tile_mask, frame_order.reshape(1, -1))])
 
 
-def share_kernel(stat_own, stat_ref, send, recv):
+def share_kernel(qg_mine, stat_own, dq_ref, qg_ref, stat_ref, dq_got, stat_send, stat_recv, pair_send, pair_recv,
+                 core_send, core_recv):
     place = Place()
-    peers = [(o, c) for o in ALL_OFFSETS for c in (0, 1)][1:]
-
-    wait_all = greet([place.mirror_device(*p) for p in peers])
+    peers = [(o, c) for o in OFFSETS for c in (0, 1)] + [((0, 0, 0), 1)]
+    wait_all = greet(
+        [place.mirror_device(*p) for p in peers] + [place.pair_device(o) for o in OFFSETS]
+    )
     own = place.block()
     stat_ref[own] = stat_own[...]
+    for offset in ALL_OFFSETS:
+        qg_ref[place.block(offset)] = qg_mine[place.block(offset)]
+
+    def core_copy(i, arriving=False):
+        block = place.block(ALL_OFFSETS[i], int(arriving))
+        return remote(qg_mine.at[block], qg_ref.at[block], core_send.at[i], core_recv.at[i],
+                      place.mirror_device((0, 0, 0), 1))
 
     def stat_copy(i, arriving=False):
         offset, flip = peers[i]
         source = place.block(offset, flip) if arriving else own
         part = stat_ref.at[source]
-        return remote(part, part, send.at[i], recv.at[i], place.mirror_device(offset, flip))
+        return remote(part, part, stat_send.at[i], stat_recv.at[i], place.mirror_device(offset, flip))
+
+    def pair_copy(i, arriving=False):
+        landing = dq_got.at[place.head(OFFSETS[i]) if arriving else place.head()]
+        return remote(dq_ref.at[place.entry(OFFSETS[i])], landing, pair_send.at[i], pair_recv.at[i],
+                      place.pair_device(OFFSETS[i]))
 
     wait_all()
     for i in range(15):
         stat_copy(i).start()
+    for i in range(7):
+        pair_copy(i).start()
+    for i in range(8):
+        core_copy(i).start()
+    dq_got[place.head()] = dq_ref[place.entry()]
+    for i in range(8):
+        core_copy(i, True).wait_recv()
     for i in range(15):
         stat_copy(i, True).wait_recv()
+    for i in range(7):
+        pair_copy(i, True).wait_recv()
+    for i in range(8):
+        core_copy(i).wait_send()
     for i in range(15):
         stat_copy(i).wait_send()
-
-
-def share(stat_own):
+    for i in range(7):
+        pair_copy(i).wait_send()
+
+
+def share(qg_mine, stat_own, dq):
     return pl.pallas_call(
         share_kernel,
         name="share",
-        out_shape=jax.ShapeDtypeStruct((BLOCKS, 8, LANES), F32),
-        in_specs=[VMEM_SPEC],
-        out_specs=VMEM_SPEC,
-        scratch_shapes=[pltpu.SemaphoreType.DMA((15,)), pltpu.SemaphoreType.DMA((15,))],
+        out_shape=(
+            jax.ShapeDtypeStruct((BLOCKS, BLOCK, LANES), BF16),
+            jax.ShapeDtypeStruct((BLOCKS, 8, LANES), F32),
+            jax.ShapeDtypeStruct((HEADS, ROWS // 2, LANES), BF16),
+        ),
+        in_specs=[VMEM_SPEC] * 3,
+        out_specs=(VMEM_SPEC,) * 3,
+        scratch_shapes=[
+            pltpu.SemaphoreType.DMA((15,)),
+            pltpu.SemaphoreType.DMA((15,)),
+            pltpu.SemaphoreType.DMA((7,)),
+            pltpu.SemaphoreType.DMA((7,)),
+            pltpu.SemaphoreType.DMA((8,)),
+            pltpu.SemaphoreType.DMA((8,)),
+        ],
         compiler_params=pltpu.CompilerParams(
-            collective_id=1, has_side_effects=True, vmem_limit_bytes=4 * 2**20
+            collective_id=1, has_side_effects=True, vmem_limit_bytes=8 * 2**20
         ),
-    )(stat_own)
+    )(qg_mine, stat_own, dq)
 
 
 def query_kernel(kv_ref, qg_own, list_ref, stat_ref, dq_ref, term_buf, peak_buf, stat_buf):
@@ -530,29 +577,23 @@
     )(qg.reshape(SLOTS, TILE, LANES), stats, kv_own.reshape(TILES, TILE, LANES), lists)
 
 
-def leave_kernel(dq_ref, dkv_ref, dq_got, dkv_got, pair_send, pair_recv):
+def leave_kernel(dkv_ref, dkv_got, pair_send, pair_recv):
     place = Place()
     wait_all = greet([place.pair_device(o) for o in OFFSETS])
-    mine = place.head()
-    sources, landings = (dq_ref, dkv_ref), (dq_got, dkv_got)
-
-    def pair_copy(which, i, arriving=False):
-        landing = landings[which].at[place.head(OFFSETS[i]) if arriving else mine]
-        return remote(sources[which].at[place.entry(OFFSETS[i])], landing,
-                      pair_send.at[which, i], pair_recv.at[which, i], place.pair_device(OFFSETS[i]))
+
+    def pair_copy(i, arriving=False):
+        landing = dkv_got.at[place.head(OFFSETS[i]) if arriving else place.head()]
+        return remote(dkv_ref.at[place.entry(OFFSETS[i])], landing, pair_send.at[i], pair_recv.at[i],
+                      place.pair_device(OFFSETS[i]))
 
     wait_all()
-    for which in (0, 1):
-        for i in range(7):
-            pair_copy(which, i).start()
-    dq_got[mine] = dq_ref[place.entry()]
-    dkv_got[mine] = dkv_ref[place.entry()]
-    for which in (0, 1):
-        for i in range(7):
-            pair_copy(which, i, True).wait_recv()
-    for which in (0, 1):
-        for i in range(7):
-            pair_copy(which, i).wait_send()
+    for i in range(7):
+        pair_copy(i).start()
+    dkv_got[place.head()] = dkv_ref[place.entry()]
+    for i in range(7):
+        pair_copy(i, True).wait_recv()
+    for i in range(7):
+        pair_copy(i).wait_send()
 
 
 def unpack_kernel(dq_got, dkv_got, q_ref, k_ref, v_ref, q_out, k_out, v_out, sems):
@@ -578,21 +619,18 @@
         copy.wait()
 
 
-def leave(dq, dkv):
-    got = pl.pallas_call(
+def leave(dq_got, dkv):
+    dkv_got = pl.pallas_call(
         leave_kernel,
         name="leave",
-        out_shape=(
-            jax.ShapeDtypeStruct((HEADS, ROWS // 2, LANES), BF16),
-            jax.ShapeDtypeStruct((HEADS, ROWS, LANES), BF16),
-        ),
-        in_specs=[VMEM_SPEC] * 2,
-        out_specs=(VMEM_SPEC,) * 2,
-        scratch_shapes=[pltpu.SemaphoreType.DMA((2, 7)), pltpu.SemaphoreType.DMA((2, 7))],
+        out_shape=jax.ShapeDtypeStruct((HEADS, ROWS, LANES), BF16),
+        in_specs=[VMEM_SPEC],
+        out_specs=VMEM_SPEC,
+        scratch_shapes=[pltpu.SemaphoreType.DMA((7,)), pltpu.SemaphoreType.DMA((7,))],
         compiler_params=pltpu.CompilerParams(
             collective_id=2, has_side_effects=True, vmem_limit_bytes=8 * 2**20
         ),
-    )(dq, dkv.reshape(HEADS, ROWS, LANES))
+    )(dkv.reshape(HEADS, ROWS, LANES))
     shape = (ROWS, HEADS * HDIM)
     return pl.pallas_call(
         unpack_kernel,
@@ -602,14 +640,14 @@
         out_specs=(HBM_SPEC,) * 3,
         scratch_shapes=[pltpu.VMEM(shape, BF16)] * 3 + [pltpu.SemaphoreType.DMA((3,))],
         compiler_params=pltpu.CompilerParams(vmem_limit_bytes=8 * 2**20),
-    )(*got)
+    )(dq_got, dkv_got)
 
 
 def body(queries, keys, values, out_grad, tile_mask, frame_order):
-    kv, qg, kv_own, qg_own, lists = enter(queries, keys, values, out_grad, tile_mask, frame_order)
+    kv, qg_mine, kv_own, qg_own, lists = enter(queries, keys, values, out_grad, tile_mask, frame_order)
     stats_own, dq = query_side(kv, qg_own, lists)
-    dkv = key_side(qg, share(stats_own), kv_own, lists)
-    return leave(dq, dkv)
+    qg, stats, dq_got = share(qg_mine, stats_own, dq)
+    return leave(dq_got, key_side(qg, stats, kv_own, lists))
 
 
 def solution(mesh):

time: 57.9 us -> 59.4 us (1.026)
  Pallas kernels: 57 us -> 58.6 us
    pallas_call x2, Pallas kernels: 16.9 us -> 19.5 us  [the longest x1 13.7 us: share(): pl.pallas_call(share_kernel, name='share', out_shape=(jax.ShapeDtypeStruc...]
    pallas_call x1, Pallas kernels: 28.7 us -> 27.7 us  [enter(): pl.pallas_call(enter_kernel, name='enter', out_shape=(jax.ShapeDtypeStruc...]
where the time goes in v4:
time: 59.4 us; the launch traced here: 59.2 us
  Pallas kernels  58.6 us (99%)
  between operations  0.66 us (1%)
    pallas_call x1, Pallas kernels, enter(): pl.pallas_call(enter_kernel, name='enter', out_shape=(jax.ShapeDtypeStruc...  27.7 us
    pallas_call x1, Pallas kernels, share(): pl.pallas_call(share_kernel, name='share', out_shape=(jax.ShapeDtypeStruc...  13.7 us
    pallas_call x1, Pallas kernels, query_side(): pl.pallas_call(query_kernel, name='query_side', out_shape=(jax.ShapeDtype...  6.2 us
    pallas_call x1, Pallas kernels, leave(): pl.pallas_call(leave_kernel, name='leave', out_shape=jax.ShapeDtypeStruct...  5.8 us
    pallas_call x1, Pallas kernels, key_side(): pl.pallas_call(key_kernel, name='key_side', out_shape=jax.ShapeDtypeStruc...  4.35 us

profile of v4, /device:TPU:0, one launch (start us, length us, event | category | flops | bytes accessed | tf_op | source)
XLA Modules:
  0.0 59.2 jit_solution(15211398901173418953)
XLA Ops:
  0.6 27.7 %enter.1 = (bf16[16,512,128]{2,1,0:T(8,128)(2,1)S(1)}, bf16[16,512,128]{2,1,0:T(8,128)(2,1)S(1)}, bf16[512,128]{1,0:T(8,128)(2,1)S(1)}, bf16[512,128]{1,0:T(8,128)(2,1)S(1)}, s32[8,128]{1,0:T(8,128)S(1)}) custom-call(bf16[64,512]{1,0:T(8,128)(2,1)} %q_ref.1, bf16[64,512]{1,0:T(8,128)(2,1)} %k_ref.1, bf16[64,512]{1,0:T(8,128)(2,1)} %v_ref.1, ...), custom_call_target="tpu_custom_call" | custom-call | tf_op jit(solution)/shard_map/enter/pallas_call | solution.py:298
  28.4 6.2 %query_side.1 = (f32[8,128]{1,0:T(8,128)S(1)}, bf16[8,32,128]{2,1,0:T(8,128)(2,1)S(1)}) custom-call(bf16[64,128,128]{2,1,0:T(8,128)(2,1)S(1)} %bitcast.7, bf16[4,128,128]{2,1,0:T(8,128)(2,1)S(1)} %bitcast.10, s32[8,128]{1,0:T(8,128)S(1)} %get-tuple-element.16.list_ref), custom_call_target="tpu_custom_call" | custom-call | tf_op jit(solution)/shard_map/query_side/pallas_call | solution.py:502
  34.6 13.7 %share.1 = (bf16[16,512,128]{2,1,0:T(8,128)(2,1)S(1)}, f32[16,8,128]{2,1,0:T(8,128)S(1)}, bf16[8,32,128]{2,1,0:T(8,128)(2,1)S(1)}) custom-call(bf16[16,512,128]{2,1,0:T(8,128)(2,1)S(1)} %get-tuple-element.13.qg_mine, f32[8,128]{1,0:T(8,128)S(1)} %get-tuple-element.17.stat_own, bf16[8,32,128]{2,1,0:T(8,128)(2,1)S(1)} %get-tuple-element.18.dq_ref), custom_call_target="tpu_custom_call" | custom-call | tf_op jit(solution)/shard_map/share/pallas_call | solution.py:376
  48.2 4.3 %key_side.1 = bf16[4,128,128]{2,1,0:T(8,128)(2,1)S(1)} custom-call(bf16[64,128,128]{2,1,0:T(8,128)(2,1)S(1)} %bitcast.6, f32[16,8,128]{2,1,0:T(8,128)S(1)} %get-tuple-element.21.stat_ref, bf16[4,128,128]{2,1,0:T(8,128)(2,1)S(1)} %bitcast.9, s32[8,128]{1,0:T(8,128)S(1)} %get-tuple-element.16.list_ref), custom_call_target="tpu_custom_call" | custom-call | tf_op jit(solution)/shard_map/key_side/pallas_call | solution.py:567
  52.6 5.8 %leave.1.dkv_got = bf16[8,64,128]{2,1,0:T(8,128)(2,1)S(1)} custom-call(bf16[8,64,128]{2,1,0:T(8,128)(2,1)S(1)} %bitcast.8), custom_call_target="tpu_custom_call" | custom-call | tf_op jit(solution)/shard_map/leave/pallas_call | solution.py:623
  58.4 0.8 %unpack.1 = (bf16[64,512]{1,0:T(8,128)(2,1)}, bf16[64,512]{1,0:T(8,128)(2,1)}, bf16[64,512]{1,0:T(8,128)(2,1)}) custom-call(bf16[8,32,128]{2,1,0:T(8,128)(2,1)S(1)} %get-tuple-element.19.dq_got, bf16[8,64,128]{2,1,0:T(8,128)(2,1)S(1)} %leave.1.dkv_got), custom_call_target="tpu_custom_call" | custom-call | tf_op jit(solution)/shard_map/unpack/pallas_call | solution.py:635

commit v5 on v4

--- a/solution.py
+++ b/solution.py
@@ -16,8 +16,9 @@
 BLOCK = TILES * TILE
 BLOCKS = 16
 SLOTS = BLOCKS * TILES
-GROUP = 24
-KEY_GROUP = 24
+FIRST = 24
+GROUP = 8
+KEY_GROUP = 8
 SPAN = 4
 KEY_SPAN = 4
 PIECES = ((0, 176), (176, 176), (352, 160))
@@ -408,35 +409,41 @@
         tiles = [first * SPAN + i for i in span]
         counts = [list_ref[t, LANES - 1] for t in tiles]
         most = functools.reduce(jnp.maximum, counts)
-        steps = (most + GROUP - 1) // GROUP
+        steps = (jnp.maximum(most - FIRST, 0) + GROUP - 1) // GROUP
         both = [qg_own[t] for t in tiles]
 
-        def keys_of(i, step):
-            return jnp.concatenate([kv_ref[list_ref[tiles[i], step * GROUP + u]] for u in range(GROUP)], axis=0)
+        def over_list(work, state):
+            state = work(0, 0, FIRST, state)
+            return lax.fori_loop(
+                0, steps, lambda step, state: work(step + 1, FIRST + step * GROUP, GROUP, state), state
+            )
+
+        def keys_of(i, begin, group):
+            return jnp.concatenate([kv_ref[list_ref[tiles[i], begin + u]] for u in range(group)], axis=0)
 
         def cut(u):
             return slice(u * TILE, (u + 1) * TILE)
 
-        def term_step(step, state):
+        def term_step(step, begin, group, state):
             after = []
             for i in span:
                 before, mass = state[2 * i : 2 * i + 2]
                 query = jnp.where(low, both[i], zero)
-                scores = lax.dot_general(query, keys_of(i, step), NT, preferred_element_type=F32)
+                scores = lax.dot_general(query, keys_of(i, begin, group), NT, preferred_element_type=F32)
                 peak = before
-                for u in range(GROUP):
+                for u in range(group):
                     peak = jnp.maximum(peak, scores[:, cut(u)])
                 mass = mass * jnp.exp(before - peak)
-                for u in range(GROUP):
-                    less = jnp.where(step * GROUP + u < counts[i], 0.0, BIG).astype(F32)
+                for u in range(group):
+                    less = jnp.where(begin + u < counts[i], 0.0, BIG).astype(F32)
                     term = jnp.exp(scores[:, cut(u)] - (peak + less))
-                    term_buf[i, step, :, cut(u)] = term
+                    term_buf[i, begin + u] = term
                     mass = mass + term
                 peak_buf[i, step] = peak
                 after += [peak, mass]
             return tuple(after)
 
-        state = lax.fori_loop(0, steps, term_step, (jnp.full((TILE, LANES), -BIG, F32), zeros) * SPAN)
+        state = over_list(term_step, (jnp.full((TILE, LANES), -BIG, F32), zeros) * SPAN)
         peaks, inverses, log_masses = [], [], []
         for i in span:
             lane_peak, lane_mass = state[2 * i : 2 * i + 2]
@@ -446,40 +453,40 @@
             inverses.append(1.0 / mass)
             log_masses.append(peak + jnp.log(mass))
 
-        def out_step(step, outs):
+        def out_step(step, begin, group, outs):
             after = []
             for i in span:
                 factor = jnp.exp(peak_buf[i, step] - peaks[i]) * inverses[i]
                 peak_buf[i, step] = factor
-                probs = [(term_buf[i, step, :, cut(u)] * factor).astype(BF16) for u in range(GROUP)]
+                probs = [(term_buf[i, begin + u] * factor).astype(BF16) for u in range(group)]
                 after.append(outs[i] + lax.dot_general(
-                    jnp.concatenate(probs, axis=1), keys_of(i, step), NN, preferred_element_type=F32
+                    jnp.concatenate(probs, axis=1), keys_of(i, begin, group), NN, preferred_element_type=F32
                 ))
             return tuple(after)
 
-        outs = lax.fori_loop(0, steps, out_step, (zeros,) * SPAN)
+        outs = over_list(out_step, (zeros,) * SPAN)
         deltas = []
         for i in span:
             out = outs[i].astype(BF16).astype(F32)
             deltas.append(jnp.sum(jnp.where(low, 0.0, both[i].astype(F32) * out), axis=1, keepdims=True))
 
-        def grad_step(step, accs):
+        def grad_step(step, begin, group, accs):
             after = []
             for i in span:
-                keys = keys_of(i, step)
+                keys = keys_of(i, begin, group)
                 factor = peak_buf[i, step]
                 grad = jnp.where(low, zero, both[i])
                 prob_grad = lax.dot_general(grad, keys, NT, preferred_element_type=F32)
                 score_grad = [
-                    ((term_buf[i, step, :, cut(u)] * factor) * (prob_grad[:, cut(u)] - deltas[i])).astype(BF16)
-                    for u in range(GROUP)
+                    ((term_buf[i, begin + u] * factor) * (prob_grad[:, cut(u)] - deltas[i])).astype(BF16)
+                    for u in range(group)
                 ]
                 after.append(accs[i] + lax.dot_general(
                     jnp.concatenate(score_grad, axis=1), keys, NN, preferred_element_type=F32
                 ))
             return tuple(after)
 
-        accs = lax.fori_loop(0, steps, grad_step, (zeros,) * SPAN)
+        accs = over_list(grad_step, (zeros,) * SPAN)
         low_part = low_lanes(ROWS // 2)
         stats = stat_buf[...]
         for i in span:
@@ -509,11 +516,11 @@
         in_specs=[VMEM_SPEC, VMEM_SPEC, SMEM_SPEC],
         out_specs=(VMEM_SPEC,) * 2,
         scratch_shapes=[
-            pltpu.VMEM((SPAN, -(-SLOTS // GROUP), TILE, GROUP * TILE), F32),
-            pltpu.VMEM((SPAN, -(-SLOTS // GROUP), TILE, LANES), F32),
+            pltpu.VMEM((SPAN, SLOTS + GROUP, TILE, TILE), F32),
+            pltpu.VMEM((SPAN, SLOTS // GROUP, TILE, LANES), F32),
             pltpu.VMEM((TILE, LANES), F32),
         ],
-        compiler_params=pltpu.CompilerParams(vmem_limit_bytes=24 * 2**20),
+        compiler_params=pltpu.CompilerParams(vmem_limit_bytes=34 * 2**20),
     )(kv.reshape(SLOTS, TILE, LANES), qg_own.reshape(TILES, TILE, LANES), lists)
 
 
@@ -573,7 +580,7 @@
         scratch_shapes=[
             pltpu.VMEM((SLOTS, 8, LANES), F32),
         ],
-        compiler_params=pltpu.CompilerParams(vmem_limit_bytes=24 * 2**20),
+        compiler_params=pltpu.CompilerParams(vmem_limit_bytes=34 * 2**20),
     )(qg.reshape(SLOTS, TILE, LANES), stats, kv_own.reshape(TILES, TILE, LANES), lists)
 
 

time: 59.4 us -> 55.4 us (0.933)
  Pallas kernels: 58.6 us -> 54.5 us
    pallas_call x1, Pallas kernels: 13.7 us -> 9.77 us  [share(): pl.pallas_call(share_kernel, name='share', out_shape=(jax.ShapeDtypeStruc...]
where the time goes in v5:
time: 55.4 us; the launch traced here: 55.2 us
  Pallas kernels  54.5 us (98%)
  between operations  0.66 us (1%)
    pallas_call x1, Pallas kernels, enter(): pl.pallas_call(enter_kernel, name='enter', out_shape=(jax.ShapeDtypeStruc...  27.7 us
    pallas_call x1, Pallas kernels, share(): pl.pallas_call(share_kernel, name='share', out_shape=(jax.ShapeDtypeStruc...  9.77 us
    pallas_call x1, Pallas kernels, query_side(): pl.pallas_call(query_kernel, name='query_side', out_shape=(jax.ShapeDtype...  5.83 us
    pallas_call x1, Pallas kernels, leave(): pl.pallas_call(leave_kernel, name='leave', out_shape=jax.ShapeDtypeStruct...  5.8 us
    pallas_call x1, Pallas kernels, key_side(): pl.pallas_call(key_kernel, name='key_side', out_shape=jax.ShapeDtypeStruc...  4.58 us

profile of v5, /device:TPU:0, one launch (start us, length us, event | category | flops | bytes accessed | tf_op | source)
XLA Modules:
  0.0 55.2 jit_solution(18025998021552303307)
XLA Ops:
  0.6 27.7 %enter.1 = (bf16[16,512,128]{2,1,0:T(8,128)(2,1)S(1)}, bf16[16,512,128]{2,1,0:T(8,128)(2,1)S(1)}, bf16[512,128]{1,0:T(8,128)(2,1)S(1)}, bf16[512,128]{1,0:T(8,128)(2,1)S(1)}, s32[8,128]{1,0:T(8,128)S(1)}) custom-call(bf16[64,512]{1,0:T(8,128)(2,1)} %q_ref.1, bf16[64,512]{1,0:T(8,128)(2,1)} %k_ref.1, bf16[64,512]{1,0:T(8,128)(2,1)} %v_ref.1, ...), custom_call_target="tpu_custom_call" | custom-call | tf_op jit(solution)/shard_map/enter/pallas_call | solution.py:299
  28.4 5.8 %query_side.1 = (f32[8,128]{1,0:T(8,128)S(1)}, bf16[8,32,128]{2,1,0:T(8,128)(2,1)S(1)}) custom-call(bf16[64,128,128]{2,1,0:T(8,128)(2,1)S(1)} %bitcast.7, bf16[4,128,128]{2,1,0:T(8,128)(2,1)S(1)} %bitcast.10, s32[8,128]{1,0:T(8,128)S(1)} %get-tuple-element.16.list_ref), custom_call_target="tpu_custom_call" | custom-call | tf_op jit(solution)/shard_map/query_side/pallas_call | solution.py:509
  34.2 9.8 %share.1 = (bf16[16,512,128]{2,1,0:T(8,128)(2,1)S(1)}, f32[16,8,128]{2,1,0:T(8,128)S(1)}, bf16[8,32,128]{2,1,0:T(8,128)(2,1)S(1)}) custom-call(bf16[16,512,128]{2,1,0:T(8,128)(2,1)S(1)} %get-tuple-element.13.qg_mine, f32[8,128]{1,0:T(8,128)S(1)} %get-tuple-element.17.stat_own, bf16[8,32,128]{2,1,0:T(8,128)(2,1)S(1)} %get-tuple-element.18.dq_ref), custom_call_target="tpu_custom_call" | custom-call | tf_op jit(solution)/shard_map/share/pallas_call | solution.py:377
  44.0 4.6 %key_side.1 = bf16[4,128,128]{2,1,0:T(8,128)(2,1)S(1)} custom-call(bf16[64,128,128]{2,1,0:T(8,128)(2,1)S(1)} %bitcast.6, f32[16,8,128]{2,1,0:T(8,128)S(1)} %get-tuple-element.21.stat_ref, bf16[4,128,128]{2,1,0:T(8,128)(2,1)S(1)} %bitcast.9, s32[8,128]{1,0:T(8,128)S(1)} %get-tuple-element.16.list_ref), custom_call_target="tpu_custom_call" | custom-call | tf_op jit(solution)/shard_map/key_side/pallas_call | solution.py:574
  48.6 5.8 %leave.1.dkv_got = bf16[8,64,128]{2,1,0:T(8,128)(2,1)S(1)} custom-call(bf16[8,64,128]{2,1,0:T(8,128)(2,1)S(1)} %bitcast.8), custom_call_target="tpu_custom_call" | custom-call | tf_op jit(solution)/shard_map/leave/pallas_call | solution.py:630
  54.4 0.8 %unpack.1 = (bf16[64,512]{1,0:T(8,128)(2,1)}, bf16[64,512]{1,0:T(8,128)(2,1)}, bf16[64,512]{1,0:T(8,128)(2,1)}) custom-call(bf16[8,32,128]{2,1,0:T(8,128)(2,1)S(1)} %get-tuple-element.19.dq_got, bf16[8,64,128]{2,1,0:T(8,128)(2,1)S(1)} %leave.1.dkv_got), custom_call_target="tpu_custom_call" | custom-call | tf_op jit(solution)/shard_map/unpack/pallas_call | solution.py:642
